TPU v7x, 256 devices: a whole 4x4x8 slice. The times are simulated.
256 devices in a mesh: gx: 4 (over y_lo, core), gy: 8 (over z), gz: 8 (over y_hi, x).
Axes of the slice: x: 4, y: 4 (y_hi: 2, y_lo: 2; y = y_hi * 2 + y_lo), z: 8, core: 2. Of those that a mesh axis runs over, the one named last changes fastest.
Arguments:
- block: float32 [32, 64, 64, 256], P('gx', 'gy', 'gz'), may hold values from -8 to 8
- onsite: float32 [32, 64, 64], P('gx', 'gy', 'gz'), may hold values from -8 to 8
- hopping: float32 [13], replicated, may hold values from -1 to 1
- cut_frac: float32 [1], replicated, may hold values from -0.5 to 0
Outputs:
- states: float32 [32, 64, 64, 256], P('gx', 'gy', 'gz')
- projected: float32 [256, 256], replicated
- factor: float32 [256, 256], replicated
All inputs are finite; a program needn't handle non-finite values. Where the computation divides by a largest or mean magnitude, that divisor is 1e-20 or more.
Results may differ from a plain program's by a relative error of at most 0.0008.
Values sent between devices are 32-bit elements; how exact they have to be, the bound alone decides.
A program may use at most 64 MiB of HBM per device.

v0:
```python
import jax
import jax.numpy as jnp
from jax import lax
from jax.sharding import PartitionSpec as P

DEG = 4


def extended(block, sides, width):
    for axis, dim in sides:
        count = lax.axis_size(axis)
        forward = [(i, i + 1) for i in range(count - 1)]
        backward = [(target, source) for source, target in forward]
        low = lax.ppermute(
            lax.slice_in_dim(block, block.shape[dim] - width, None, axis=dim), axis, forward
        )
        high = lax.ppermute(lax.slice_in_dim(block, 0, width, axis=dim), axis, backward)
        block = jnp.concatenate([low, block, high], axis=dim)
    return block


def half_offsets():
    result = []
    for dx in (-1, 0, 1):
        for dy in (-1, 0, 1):
            for dz in (-1, 0, 1):
                if (dx, dy, dz) > (0, 0, 0):
                    result.append((dx, dy, dz))
    return result


def stencil(padded, field, onsite, hopping):
    size_x, size_y, size_z = (field.shape[0], field.shape[1], field.shape[2])
    total = onsite[:, :, :, None] * field
    for index, offset in enumerate(half_offsets()):
        for sign in (1, -1):
            ax_x, ax_y, ax_z = (1 + sign * offset[0], 1 + sign * offset[1], 1 + sign * offset[2])
            total = (
                total
                + hopping[index]
                * padded[ax_x : ax_x + size_x, ax_y : ax_y + size_y, ax_z : ax_z + size_z]
            )
    return total


def apply_ham(field, onsite, hopping):
    padded = extended(field, (("gx", 0), ("gy", 1), ("gz", 2)), 1)
    return stencil(padded, field, onsite, hopping)


def cheb_filter(field, operate, bound, cut):
    half_width = (bound - cut) / 2.0
    center = (bound + cut) / 2.0
    sigma = half_width / (-bound - center)
    sigma_one = sigma
    older = field
    newer = sigma / half_width * (operate(older) - center * older)
    for step in range(DEG - 1):
        sigma_next = 1.0 / (2.0 / sigma_one - sigma)
        nextone = (
            2.0 * sigma_next / half_width * (operate(newer) - center * newer)
            - sigma * sigma_next * older
        )
        older, newer, sigma = (newer, nextone, sigma_next)
    return newer


def gram_of(left, right):
    return lax.dot_general(
        left,
        right,
        (((0,), (0,)), ((), ())),
        precision=lax.Precision.HIGHEST,
        preferred_element_type=jnp.float32,
    )


def lower_and_inverse(gram):
    lower = jnp.linalg.cholesky(gram)
    ident = jnp.eye(gram.shape[0], dtype=jnp.float32)
    return (lower, jax.scipy.linalg.solve_triangular(lower, ident, lower=True))


def rotate(flat, factor):
    return jnp.dot(
        flat, factor.T, precision=lax.Precision.HIGHEST, preferred_element_type=jnp.float32
    )


def body(block, onsite, hopping, cut_frac):
    shape = block.shape
    size_x, size_y, size_z, columns = shape
    total_sites = (
        size_x * size_y * size_z * lax.axis_size("gx") * lax.axis_size("gy") * lax.axis_size("gz")
    )
    largest = lax.pmax(jnp.max(jnp.abs(onsite)), ("gx", "gy", "gz"))
    bound = largest + 2.0 * jnp.sum(jnp.abs(hopping))
    cut = cut_frac[0] * bound
    filtered = cheb_filter(block, lambda field: apply_ham(field, onsite, hopping), bound, cut)
    flat = filtered.reshape(-1, columns)
    gram_one = lax.psum(gram_of(flat, flat), ("gx", "gy", "gz")) / total_sites
    lower_one, inverse_one = lower_and_inverse(gram_one)
    first = rotate(flat, inverse_one)
    gram_two = lax.psum(gram_of(first, first), ("gx", "gy", "gz")) / total_sites
    lower_two, factor_two = lower_and_inverse(gram_two)
    states = rotate(first, factor_two)
    image = apply_ham(states.reshape(shape), onsite, hopping).reshape(-1, columns)
    projected = lax.psum(gram_of(states, image), ("gx", "gy", "gz")) / total_sites
    return (states.reshape(shape), projected, lower_one)


def solution(mesh):
    return jax.shard_map(
        body,
        mesh=mesh,
        in_specs=(P("gx", "gy", "gz", None), P("gx", "gy", "gz"), P(), P()),
        out_specs=(P("gx", "gy", "gz", None), P(), P()),
        check_vma=False,
    )
```

profile of v0, /device:TPU:1, one launch (start us, length us, event | category | flops | bytes accessed | tf_op | source)
XLA Modules:
  0.0 1180.3 jit_solution(2709486755815399544)
XLA Ops:
  8.1 4.6 collective-permute-start
  16.0 79.4 %pmax.7 = f32[]{:T(128)} all-reduce(f32[]{:T(128)} %abs_reduce_fusion), channel_id=1, replica_groups=mesh['gx'=4,'gy'=8,'gz'=8] {'gx','gy','gz'}, use_global_device_ids=true, to_apply=%region_1.0 | all-reduce | flops 1 | bytes 8 | tf_op jit(solution)/shard_map/pmax | solution.py:96
  98.6 4.0 collective-permute-start.2
  106.0 4.0 collective-permute-start.5
  112.1 10.0 fusion.160
  122.1 4.3 collective-permute-start.7
  131.0 4.6 collective-permute-start.8
  138.8 4.7 collective-permute-start.11
  145.6 10.0 fusion.124
  165.9 4.6 collective-permute-start.14
  173.4 4.7 collective-permute-start.17
  180.7 10.0 fusion.93
  192.7 5.5 collective-permute-start.18
  200.8 4.6 collective-permute-start.20
  208.4 4.7 collective-permute-start.23
  215.2 10.0 fusion.62
  227.5 270.7 %all-reduce.5.cloned.1.call-done = f32[256,256]{0,1:T(8,128)} async-done(((f32[256,256]{0,1:T(8,128)}), f32[256,256]{0,1:T(8,128)}) %all-reduce.5.cloned.1.call-update) | async-done | bytes 262160 | tf_op jit(solution)/shard_map/psum | solution.py:101
  500.3 11.7 cholesky.130
  512.0 9.8 custom-call.13
  522.3 11.7 cholesky.147
  536.9 4.0 while.4
  540.9 19.7 %custom-call.14 = f32[2,128,128]{1,2,0:T(8,128)S(1)} custom-call(f32[2,128,128]{2,1,0:T(8,128)S(1)} %get-tuple-element.19), custom_call_target="InvertDiagBlocksLowerTriangular" | custom-call | tf_op jit(solution)/shard_map/jit(_solve_triangular)/triangular_solve | solution.py:81
  563.9 249.0 %all-reduce.7.cloned.1.call-done = f32[256,256]{0,1:T(8,128)} async-done(((f32[256,256]{0,1:T(8,128)}), f32[256,256]{0,1:T(8,128)}) %all-reduce.7.cloned.1.call-update) | async-done | bytes 262160 | tf_op jit(solution)/shard_map/psum | solution.py:104
  815.0 11.7 cholesky.164
  826.8 9.8 custom-call.15
  837.1 11.7 cholesky.181
  851.4 4.1 while.5
  855.4 19.7 %custom-call.16 = f32[2,128,128]{1,2,0:T(8,128)S(1)} custom-call(f32[2,128,128]{2,1,0:T(8,128)S(1)} %get-tuple-element.20), custom_call_target="InvertDiagBlocksLowerTriangular" | custom-call | tf_op jit(solution)/shard_map/jit(_solve_triangular)/triangular_solve | solution.py:81
  886.2 4.0 collective-permute-start.26
  893.6 4.0 collective-permute-start.29
  899.7 10.0 fusion.31
  911.4 260.3 %all-reduce.9.cloned.1.call-done = f32[256,256]{0,1:T(8,128)} async-done(((f32[256,256]{0,1:T(8,128)}), f32[256,256]{0,1:T(8,128)}) %all-reduce.9.cloned.1.call-update) | async-done | bytes 262160 | tf_op jit(solution)/shard_map/psum | solution.py:108
  (144 shorter events, 86.5 us)
Async XLA Ops:
  7.2 491.0 %all-reduce.5.cloned.1.call-start = ((), (), s32[]{:S(2)}) async-start(), calls=%async_computation | async-start | bytes 524288 | tf_op jit(solution)/shard_map/psum | solution.py:101
  8.1 88.0 %collective-permute-start = (f32[1,8,8,256]{3,2,1,0:T(8,128)S(1)}, f32[1,8,8,256]{3,2,1,0:T(8,128)S(1)}, u32[]{:S(2)}, u32[]{:S(2)}) collective-permute-start(f32[1,8,8,256]{3,2,1,0:T(8,128)S(1)} %get-tuple-element.93), channel_id=1, source_target_pairs={{0,64},{64,128},{128,192},{1,65},{65,129},{129,193},{2,66},{66,130... | collective-permute-start | bytes 196616 | tf_op jit(solution)/shard_map/ppermute | solution.py:14
  14.1 83.1 %collective-permute-start.1 = (f32[1,8,8,256]{3,2,1,0:T(8,128)S(1)}, f32[1,8,8,256]{3,2,1,0:T(8,128)S(1)}, u32[]{:S(2)}, u32[]{:S(2)}) collective-permute-start(f32[1,8,8,256]{3,2,1,0:T(8,128)S(1)} %get-tuple-element.92), channel_id=1, source_target_pairs={{64,0},{128,64},{192,128},{65,1},{129,65},{193,129},{66,2},{130,66... | collective-permute-start | bytes 196616 | tf_op jit(solution)/shard_map/ppermute | solution.py:17
  97.3 7.3 collective-permute-start.3
  98.6 6.0 collective-permute-start.2
  104.7 6.0 collective-permute-start.4
  106.0 5.7 collective-permute-start.5
  122.1 6.2 collective-permute-start.7
  129.7 6.8 collective-permute-start.9
  131.0 6.4 collective-permute-start.8
  137.5 6.4 collective-permute-start.10
  138.8 6.3 collective-permute-start.11
  155.7 7.6 collective-permute-start.13
  159.3 5.3 collective-permute-start.12
  164.6 6.0 collective-permute-start.15
  165.9 6.1 collective-permute-start.14
  172.1 6.3 collective-permute-start.16
  173.4 6.8 collective-permute-start.17
  190.8 7.5 collective-permute-start.19
  192.7 6.8 collective-permute-start.18
  199.5 6.0 collective-permute-start.21
  200.8 6.1 collective-permute-start.20
  207.1 6.1 collective-permute-start.22
  208.4 6.3 collective-permute-start.23
  226.9 586.0 %all-reduce.7.cloned.1.call-start = ((), (), s32[]{:S(2)}) async-start(), calls=%async_computation.1 | async-start | bytes 524288 | tf_op jit(solution)/shard_map/psum | solution.py:104
  563.8 607.9 %all-reduce.9.cloned.1.call-start = ((), (), s32[]{:S(2)}) async-start(), calls=%async_computation.2 | async-start | bytes 524288 | tf_op jit(solution)/shard_map/psum | solution.py:108
  876.7 6.9 collective-permute-start.25
  880.5 4.4 collective-permute-start.24
  884.9 5.4 collective-permute-start.27
  886.2 5.9 collective-permute-start.26
  892.3 6.2 collective-permute-start.28
  893.6 5.7 collective-permute-start.29
  (5 other events, 134.5 us)
Sparse Core Ops, SparseCore 0:
  227.1 271.0 all-reduce.4
  563.9 248.9 all-reduce.6
  911.5 260.1 all-reduce.8
where the time goes:
time: 1190 us; the launch traced here: 1180 us
  waiting for transfers between devices  799 us (67%)
  other arithmetic  169 us (14%)
  starting transfers between devices  92 us (8%)
  blocking collectives  79.4 us (7%)
  between operations  19.7 us (2%)
    psum x1, waiting for transfers between devices, body(): gram_one = lax.psum(gram_of(flat, flat), ('gx', 'gy', 'gz')) / total_sites  271 us
    psum x1, waiting for transfers between devices, body(): lax.psum(gram_of(states, image), ('gx', 'gy', 'gz')) / total_sites  260 us
    psum x1, waiting for transfers between devices, body(): gram_two = lax.psum(gram_of(first, first), ('gx', 'gy', 'gz')) / total_sites  249 us
    pmax x1, blocking collectives, body(): largest = lax.pmax(jnp.max(jnp.abs(onsite)), ('gx', 'gy', 'gz'))  79.4 us
    another operation x13, other arithmetic, lower_and_inverse(): lower = jnp.linalg.cholesky(gram)  68.5 us
    ppermute x15, starting transfers between devices, extended(): lax.ppermute(lax.slice_in_dim(block, block.shape[dim] - width, None, axis...  62.9 us
    another operation x5, other arithmetic, lower_and_inverse(): return (lower, jax.scipy.linalg.solve_triangular(lower, ident, lower=True))  40.1 us
    sub x3, other arithmetic, cheb_filter(): 2.0 * sigma_next / half_width * (operate(newer) - center * newer)  30.1 us
  transfers between devices with their start and end apart: 33, of which 21 were waited for; matrix products, arithmetic and copies ran while one was open for 0% of the time, Pallas kernels for 0%

commit v1 on v0

--- a/solution.py
+++ b/solution.py
@@ -1,9 +1,15 @@
+import functools
+
 import jax
 import jax.numpy as jnp
 from jax import lax
+from jax.experimental import pallas as pl
+from jax.experimental.pallas import tpu as pltpu
 from jax.sharding import PartitionSpec as P
 
 DEG = 4
+MESH = pl.DeviceIdType.MESH
+HIGHEST = lax.Precision.HIGHEST
 
 
 def extended(block, sides, width):
@@ -65,14 +71,172 @@
     return newer
 
 
-def gram_of(left, right):
-    return lax.dot_general(
-        left,
-        right,
+def plane_peer(dims, offset):
+    size_x, _, size_z = dims
+    place = lax.axis_index("gx") * size_z + lax.axis_index("gz")
+    peer = lax.rem(place + offset, size_x * size_z)
+    return peer, {"gx": peer // size_z, "gz": lax.rem(peer, size_z)}
+
+
+def column_peer(dims, offset):
+    peer = lax.rem(lax.axis_index("gy") + offset, dims[1])
+    return peer, {"gy": peer}
+
+
+def enter(dims):
+    barrier = pltpu.get_barrier_semaphore()
+    plane, column = dims[0] * dims[2], dims[1]
+
+    @pl.loop(1, plane)
+    def _(k):
+        pl.semaphore_signal(barrier, inc=1, device_id=plane_peer(dims, k)[1], device_id_type=MESH)
+
+    @pl.loop(1, column)
+    def _(k):
+        pl.semaphore_signal(barrier, inc=1, device_id=column_peer(dims, k)[1], device_id_type=MESH)
+
+
+def entered(dims):
+    pl.semaphore_wait(pltpu.get_barrier_semaphore(), dims[0] * dims[2] + dims[1] - 2)
+
+
+def wait_bytes(ref, sem):
+    pltpu.make_async_copy(ref, ref, sem).wait()
+
+
+def send(src, dst, send_sem, recv_sem, device):
+    pltpu.make_async_remote_copy(
+        src_ref=src,
+        dst_ref=dst,
+        send_sem=send_sem,
+        recv_sem=recv_sem,
+        device_id=device,
+        device_id_type=MESH,
+    ).start()
+
+
+def all_reduce(dims, local, total, plane_buf, column_buf, sems):
+    plane, column = dims[0] * dims[2], dims[1]
+    rows = local.shape[0] // plane
+    place = lax.axis_index("gx") * dims[2] + lax.axis_index("gz")
+    level = lax.axis_index("gy")
+    mine = pl.ds(pl.multiple_of(place * rows, rows), rows)
+
+    @pl.loop(1, plane)
+    def _(k):
+        peer, device = plane_peer(dims, k)
+        theirs = pl.ds(pl.multiple_of(peer * rows, rows), rows)
+        send(local.at[theirs], plane_buf.at[k - 1], sems.at[0], sems.at[1], device)
+
+    wait_bytes(plane_buf, sems.at[1])
+    column_buf[level] = lax.fori_loop(
+        0, plane - 1, lambda k, acc: acc + plane_buf[k], local[mine]
+    )
+
+    @pl.loop(1, column)
+    def _(k):
+        _, device = column_peer(dims, k)
+        send(column_buf.at[level], column_buf.at[level], sems.at[2], sems.at[3], device)
+
+    wait_bytes(column_buf.at[pl.ds(0, column - 1)], sems.at[3])
+    part = column_buf[0]
+    for k in range(1, column):
+        part = part + column_buf[k]
+    total[mine] = part
+
+    @pl.loop(1, plane)
+    def _(k):
+        _, device = plane_peer(dims, k)
+        send(total.at[mine], total.at[mine], sems.at[4], sems.at[5], device)
+
+    wait_bytes(total.at[pl.ds(0, (plane - 1) * rows)], sems.at[5])
+    wait_bytes(plane_buf, sems.at[0])
+    wait_bytes(column_buf.at[pl.ds(0, column - 1)], sems.at[2])
+    wait_bytes(total.at[pl.ds(0, (plane - 1) * rows)], sems.at[4])
+
+
+def reduce_scratch(dims, size):
+    plane, column = dims[0] * dims[2], dims[1]
+    rows = size // plane
+    return [
+        pltpu.VMEM((plane - 1, rows, size), jnp.float32),
+        pltpu.VMEM((column, rows, size), jnp.float32),
+        pltpu.SemaphoreType.DMA((6,)),
+    ]
+
+
+def gram_kernel(dims, sites, left, right, out, local, total, plane_buf, column_buf, sems):
+    enter(dims)
+    local[...] = lax.dot_general(
+        left[...],
+        right[...],
         (((0,), (0,)), ((), ())),
-        precision=lax.Precision.HIGHEST,
+        precision=HIGHEST,
         preferred_element_type=jnp.float32,
     )
+    entered(dims)
+    all_reduce(dims, local, total, plane_buf, column_buf, sems)
+    out[...] = total[...] / sites
+
+
+def gram_sum(dims, sites, left, right, ident):
+    size = left.shape[1]
+    vmem = pl.BlockSpec(memory_space=pltpu.VMEM)
+    return pl.pallas_call(
+        functools.partial(gram_kernel, dims, sites),
+        out_shape=jax.ShapeDtypeStruct((size, size), jnp.float32),
+        in_specs=[vmem, vmem],
+        out_specs=vmem,
+        scratch_shapes=[pltpu.VMEM((size, size), jnp.float32)] * 2 + reduce_scratch(dims, size),
+        compiler_params=pltpu.CompilerParams(
+            collective_id=ident, has_side_effects=True, vmem_limit_bytes=32 << 20
+        ),
+    )(left, right)
+
+
+def max_kernel(dims, onsite, out, plane_buf, column_buf, sems):
+    enter(dims)
+    plane, column = dims[0] * dims[2], dims[1]
+    place = lax.axis_index("gx") * dims[2] + lax.axis_index("gz")
+    level = lax.axis_index("gy")
+    plane_buf[place] = jnp.full(plane_buf.shape[1:], jnp.max(jnp.abs(onsite[...])), jnp.float32)
+    entered(dims)
+
+    @pl.loop(1, plane)
+    def _(k):
+        _, device = plane_peer(dims, k)
+        send(plane_buf.at[place], plane_buf.at[place], sems.at[0], sems.at[1], device)
+
+    wait_bytes(plane_buf.at[pl.ds(0, plane - 1)], sems.at[1])
+    column_buf[level] = jnp.max(plane_buf[...], axis=0)
+
+    @pl.loop(1, column)
+    def _(k):
+        _, device = column_peer(dims, k)
+        send(column_buf.at[level], column_buf.at[level], sems.at[2], sems.at[3], device)
+
+    wait_bytes(column_buf.at[pl.ds(0, column - 1)], sems.at[3])
+    out[...] = jnp.max(column_buf[...], axis=0)
+    wait_bytes(plane_buf.at[pl.ds(0, plane - 1)], sems.at[0])
+    wait_bytes(column_buf.at[pl.ds(0, column - 1)], sems.at[2])
+
+
+def max_all(dims, onsite):
+    vmem = pl.BlockSpec(memory_space=pltpu.VMEM)
+    plane, column = dims[0] * dims[2], dims[1]
+    out = pl.pallas_call(
+        functools.partial(max_kernel, dims),
+        out_shape=jax.ShapeDtypeStruct((8, 128), jnp.float32),
+        in_specs=[vmem],
+        out_specs=vmem,
+        scratch_shapes=[
+            pltpu.VMEM((plane, 8, 128), jnp.float32),
+            pltpu.VMEM((column, 8, 128), jnp.float32),
+            pltpu.SemaphoreType.DMA((4,)),
+        ],
+        compiler_params=pltpu.CompilerParams(collective_id=0, has_side_effects=True),
+    )(onsite.reshape(-1, onsite.shape[-1]))
+    return out[0, 0]
 
 
 def lower_and_inverse(gram):
@@ -82,36 +246,33 @@
 
 
 def rotate(flat, factor):
-    return jnp.dot(
-        flat, factor.T, precision=lax.Precision.HIGHEST, preferred_element_type=jnp.float32
-    )
-
-
-def body(block, onsite, hopping, cut_frac):
+    return jnp.dot(flat, factor.T, precision=HIGHEST, preferred_element_type=jnp.float32)
+
+
+def body(dims, block, onsite, hopping, cut_frac):
     shape = block.shape
     size_x, size_y, size_z, columns = shape
-    total_sites = (
-        size_x * size_y * size_z * lax.axis_size("gx") * lax.axis_size("gy") * lax.axis_size("gz")
-    )
-    largest = lax.pmax(jnp.max(jnp.abs(onsite)), ("gx", "gy", "gz"))
+    total_sites = size_x * size_y * size_z * dims[0] * dims[1] * dims[2]
+    largest = max_all(dims, onsite)
     bound = largest + 2.0 * jnp.sum(jnp.abs(hopping))
     cut = cut_frac[0] * bound
     filtered = cheb_filter(block, lambda field: apply_ham(field, onsite, hopping), bound, cut)
     flat = filtered.reshape(-1, columns)
-    gram_one = lax.psum(gram_of(flat, flat), ("gx", "gy", "gz")) / total_sites
+    gram_one = gram_sum(dims, total_sites, flat, flat, 1)
     lower_one, inverse_one = lower_and_inverse(gram_one)
     first = rotate(flat, inverse_one)
-    gram_two = lax.psum(gram_of(first, first), ("gx", "gy", "gz")) / total_sites
+    gram_two = gram_sum(dims, total_sites, first, first, 2)
     lower_two, factor_two = lower_and_inverse(gram_two)
     states = rotate(first, factor_two)
     image = apply_ham(states.reshape(shape), onsite, hopping).reshape(-1, columns)
-    projected = lax.psum(gram_of(states, image), ("gx", "gy", "gz")) / total_sites
+    projected = gram_sum(dims, total_sites, states, image, 3)
     return (states.reshape(shape), projected, lower_one)
 
 
 def solution(mesh):
+    dims = (mesh.shape["gx"], mesh.shape["gy"], mesh.shape["gz"])
     return jax.shard_map(
-        body,
+        functools.partial(body, dims),
         mesh=mesh,
         in_specs=(P("gx", "gy", "gz", None), P("gx", "gy", "gz"), P(), P()),
         out_specs=(P("gx", "gy", "gz", None), P(), P()),

time: 1190 us -> 426 us (0.36)
  waiting for transfers between devices: 799 us -> 20 us
  Pallas kernels: 0 us -> 121 us
  blocking collectives: 79.4 us -> 0 us
  between operations: 19.7 us -> 6.63 us
    psum x3 -> x0, waiting for transfers between devices: 780 us -> none  [the longest x1 271 us: body(): gram_one = lax.psum(gram_of(flat, flat), ('gx', 'gy', 'gz')) / total_sites]
    pallas_call x0 -> x4, Pallas kernels: none -> 121 us  [the longest x3 101 us: gram_sum(): pl.pallas_call(functools.partial(gram_kernel, dims, sites), out_shape=jax...]
    pmax x1 -> x0, blocking collectives: 79.4 us -> none  [body(): largest = lax.pmax(jnp.max(jnp.abs(onsite)), ('gx', 'gy', 'gz'))]
  transfers between devices with their start and end apart: 33 -> 30, of which waited for: 21 -> 18; matrix products, arithmetic and copies ran while one was open for 0% -> 1% of each run, Pallas kernels for 0% -> 5%
where the time goes in v1:
time: 426 us; the launch traced here: 418 us
  other arithmetic  162 us (38%)
  Pallas kernels  121 us (28%)
  starting transfers between devices  90.5 us (21%)
  waiting for transfers between devices  20 us (5%)
  local copies, waits for them, and re-layouts  13.1 us (3%)
  between operations  6.63 us (2%)
    pallas_call x3, Pallas kernels, gram_sum(): pl.pallas_call(functools.partial(gram_kernel, dims, sites), out_shape=jax...  101 us
    another operation x13, other arithmetic, lower_and_inverse(): lower = jnp.linalg.cholesky(gram)  68.7 us
    ppermute x15, starting transfers between devices, extended(): lax.ppermute(lax.slice_in_dim(block, block.shape[dim] - width, None, axis...  62.9 us
    another operation x5, other arithmetic, lower_and_inverse(): return (lower, jax.scipy.linalg.solve_triangular(lower, ident, lower=True))  40.5 us
    sub x3, other arithmetic, cheb_filter(): 2.0 * sigma_next / half_width * (operate(newer) - center * newer)  29.6 us
    ppermute x15, starting transfers between devices, extended(): lax.ppermute(lax.slice_in_dim(block, 0, width, axis=dim), axis, backward)  27.6 us
    pallas_call x1, Pallas kernels, max_all(): pl.pallas_call(functools.partial(max_kernel, dims), out_shape=jax.ShapeDt...  19.7 us
    ppermute x15, waiting for transfers between devices, extended(): lax.ppermute(lax.slice_in_dim(block, block.shape[dim] - width, None, axis...  17.2 us
  transfers between devices with their start and end apart: 30, of which 18 were waited for; matrix products, arithmetic and copies ran while one was open for 1% of the time, Pallas kernels for 5%

profile of v1, /device:TPU:1, one launch (start us, length us, event | category | flops | bytes accessed | tf_op | source)
XLA Modules:
  0.0 417.8 jit_solution(11365242143779125626)
XLA Ops:
  1.5 4.6 %collective-permute-start = (f32[1,8,8,256]{3,2,1,0:T(8,128)S(1)}, f32[1,8,8,256]{3,2,1,0:T(8,128)S(1)}, u32[]{:S(2)}, u32[]{:S(2)}) collective-permute-start(f32[1,8,8,256]{3,2,1,0:T(8,128)S(1)} %get-tuple-element.90), channel_id=1, source_target_pairs={{0,64},{64,128},{128,192},{1,65},{65,129},{129,193},{2,66},{66,130... | collective-permute-start | bytes 196616 | tf_op jit(solution)/shard_map/ppermute | solution.py:20
  8.1 19.7 %shard_map.67 = f32[8,128]{1,0:T(8,128)} custom-call(f32[64,8]{1,0:T(8,128)} %bitcast.98), custom_call_target="tpu_custom_call" | custom-call | tf_op jit(solution)/shard_map/pallas_call | solution.py:227
  32.1 4.0 collective-permute-start.2
  39.5 4.0 collective-permute-start.5
  45.6 9.8 %fusion.160 = f32[8,8,8,256]{3,2,1,0:T(8,128)S(1)} fusion(f32[8,8,8,256]{3,2,1,0:T(8,128)S(1)} %copy-done.1, f32[10,10,9,256]{3,2,1,0:T(8,128)S(1)} %get-tuple-element.60, f32[10,10,9,256]{3,2,1,0:T(8,128)S(1)} %get-tuple-element.59, f32[10,8,8,256]{3,2,1,0:T(8,128)S(1)} %constant_dynamic-update-slice_fusion, ...), kind=kLoop, calls=%fused_computation.320 | loop fusion | flops 8388608 | bytes 11438140 | tf_op jit(solution)/shard_map/mul | solution.py:63
  55.5 5.0 %collective-permute-start.7 = (f32[1,8,8,256]{3,2,1,0:T(8,128)S(1)}, f32[1,8,8,256]{3,2,1,0:T(8,128)S(1)}, u32[]{:S(2)}, u32[]{:S(2)}) collective-permute-start(f32[1,8,8,256]{3,2,1,0:T(8,128)S(1)} %get-tuple-element.88), channel_id=1, source_target_pairs={{64,0},{128,64},{192,128},{65,1},{129,65},{193,129},{66,2},{130,66... | collective-permute-start | bytes 196616 | tf_op jit(solution)/shard_map/ppermute | solution.py:23
  65.5 4.6 %collective-permute-start.8 = (f32[10,1,8,256]{3,2,1,0:T(8,128)S(1)}, f32[10,1,8,256]{3,2,1,0:T(8,128)S(1)}, u32[]{:S(2)}, u32[]{:S(2)}) collective-permute-start(f32[10,1,8,256]{3,2,1,0:T(8,128)S(1)} %get-tuple-element.77), channel_id=1, source_target_pairs={{0,8},{8,16},{16,24},{24,32},{32,40},{40,48},{48,56},{1,9},{9,17},... | collective-permute-start | bytes 245768 | tf_op jit(solution)/shard_map/ppermute | solution.py:20
  73.8 4.7 %collective-permute-start.11 = (f32[10,10,1,256]{3,2,1,0:T(1,128)S(1)}, f32[10,10,1,256]{3,2,1,0:T(1,128)S(1)}, u32[]{:S(2)}, u32[]{:S(2)}) collective-permute-start(f32[10,10,1,256]{3,2,1,0:T(1,128)S(1)} %get-tuple-element.58), channel_id=1, source_target_pairs={{0,1},{1,2},{2,3},{3,4},{4,5},{5,6},{6,7},{8,9},{9,10},{10,11},{11... | collective-permute-start | bytes 307208 | tf_op jit(solution)/shard_map/ppermute | solution.py:20
  80.8 9.9 %fusion.124 = f32[8,8,8,256]{3,2,1,0:T(8,128)S(1)} fusion(f32[10,10,9,256]{3,2,1,0:T(8,128)S(1)} %get-tuple-element.56, f32[10,10,9,256]{3,2,1,0:T(8,128)S(1)} %get-tuple-element.55, f32[10,9,8,256]{3,2,1,0:T(8,128)S(1)} %get-tuple-element.76, f32[10,9,8,256]{3,2,1,0:T(8,128)S(1)} %get-tuple-element.75, f32[8,8,8,256]{3,2,1,0:T(8,128)S(1)} %fusion.160, ...), kind=kLoop, calls=%fused_computation.237 | loop fusion | flops 7864320 | bytes 14288960 | tf_op jit(solution)/shard_map/sub | solution.py:67
  100.3 4.6 %collective-permute-start.14 = (f32[10,1,8,256]{3,2,1,0:T(8,128)S(1)}, f32[10,1,8,256]{3,2,1,0:T(8,128)S(1)}, u32[]{:S(2)}, u32[]{:S(2)}) collective-permute-start(f32[10,1,8,256]{3,2,1,0:T(8,128)S(1)} %get-tuple-element.73), channel_id=1, source_target_pairs={{0,8},{8,16},{16,24},{24,32},{32,40},{40,48},{48,56},{1,9},{9,17},... | collective-permute-start | bytes 245768 | tf_op jit(solution)/shard_map/ppermute | solution.py:20
  107.8 4.7 %collective-permute-start.17 = (f32[10,10,1,256]{3,2,1,0:T(1,128)S(1)}, f32[10,10,1,256]{3,2,1,0:T(1,128)S(1)}, u32[]{:S(2)}, u32[]{:S(2)}) collective-permute-start(f32[10,10,1,256]{3,2,1,0:T(1,128)S(1)} %get-tuple-element.54), channel_id=1, source_target_pairs={{0,1},{1,2},{2,3},{3,4},{4,5},{5,6},{6,7},{8,9},{9,10},{10,11},{11... | collective-permute-start | bytes 307208 | tf_op jit(solution)/shard_map/ppermute | solution.py:20
  115.3 9.9 %fusion.93 = f32[8,8,8,256]{3,2,1,0:T(8,128)S(1)} fusion(f32[10,10,9,256]{3,2,1,0:T(8,128)S(1)} %get-tuple-element.52, f32[10,10,9,256]{3,2,1,0:T(8,128)S(1)} %get-tuple-element.51, f32[10,9,8,256]{3,2,1,0:T(8,128)S(1)} %get-tuple-element.72, f32[10,9,8,256]{3,2,1,0:T(8,128)S(1)} %get-tuple-element.71, f32[8,8,8,256]{3,2,1,0:T(8,128)S(1)} %fusion.124, ...), kind=kLoop, calls=%fused_computation.180 | loop fusion | flops 7864320 | bytes 14288960 | tf_op jit(solution)/shard_map/sub | solution.py:67
  127.2 5.2 %collective-permute-start.18 = (f32[1,8,8,256]{3,2,1,0:T(8,128)S(1)}, f32[1,8,8,256]{3,2,1,0:T(8,128)S(1)}, u32[]{:S(2)}, u32[]{:S(2)}) collective-permute-start(f32[1,8,8,256]{3,2,1,0:T(8,128)S(1)} %get-tuple-element.83), channel_id=1, source_target_pairs={{0,64},{64,128},{128,192},{1,65},{65,129},{129,193},{2,66},{66,130... | collective-permute-start | bytes 196616 | tf_op jit(solution)/shard_map/ppermute | solution.py:20
  135.0 4.6 %collective-permute-start.20 = (f32[10,1,8,256]{3,2,1,0:T(8,128)S(1)}, f32[10,1,8,256]{3,2,1,0:T(8,128)S(1)}, u32[]{:S(2)}, u32[]{:S(2)}) collective-permute-start(f32[10,1,8,256]{3,2,1,0:T(8,128)S(1)} %get-tuple-element.69), channel_id=1, source_target_pairs={{0,8},{8,16},{16,24},{24,32},{32,40},{40,48},{48,56},{1,9},{9,17},... | collective-permute-start | bytes 245768 | tf_op jit(solution)/shard_map/ppermute | solution.py:20
  142.6 4.7 %collective-permute-start.23 = (f32[10,10,1,256]{3,2,1,0:T(1,128)S(1)}, f32[10,10,1,256]{3,2,1,0:T(1,128)S(1)}, u32[]{:S(2)}, u32[]{:S(2)}) collective-permute-start(f32[10,10,1,256]{3,2,1,0:T(1,128)S(1)} %get-tuple-element.50), channel_id=1, source_target_pairs={{0,1},{1,2},{2,3},{3,4},{4,5},{5,6},{6,7},{8,9},{9,10},{10,11},{11... | collective-permute-start | bytes 307208 | tf_op jit(solution)/shard_map/ppermute | solution.py:20
  149.4 9.9 %fusion.62 = f32[8,8,8,256]{3,2,1,0:T(8,128)S(1)} fusion(f32[10,10,9,256]{3,2,1,0:T(8,128)S(1)} %get-tuple-element.48, f32[10,10,9,256]{3,2,1,0:T(8,128)S(1)} %get-tuple-element.47, f32[10,9,8,256]{3,2,1,0:T(8,128)S(1)} %get-tuple-element.68, f32[10,9,8,256]{3,2,1,0:T(8,128)S(1)} %get-tuple-element.67, f32[8,8,8,256]{3,2,1,0:T(8,128)S(1)} %fusion.93, ...), kind=kLoop, calls=%fused_computation.123 | loop fusion | flops 7864320 | bytes 14288960 | tf_op jit(solution)/shard_map/sub | solution.py:67
  159.3 47.6 %shard_map.68 = f32[256,256]{1,0:T(8,128)S(1)} custom-call(f32[512,256]{1,0:T(8,128)S(1)} %bitcast.94, f32[512,256]{1,0:T(8,128)S(1)} %bitcast.95), custom_call_target="tpu_custom_call" | custom-call | tf_op jit(solution)/shard_map/pallas_call | solution.py:185
  207.0 11.7 %cholesky.130 = f32[128,128]{1,0:T(8,128)S(1)} custom-call(f32[128,128]{1,0:T(8,128)S(1)} %cholesky.194), custom_call_target="Cholesky" | custom-call | tf_op jit(solution)/shard_map/jit(cholesky)/cholesky | solution.py:243
  218.8 9.8 %custom-call.13 = f32[1,128,128]{1,2,0:T(8,128)S(1)} custom-call(f32[1,128,128]{2,1,0:T(8,128)S(1)} %get-tuple-element.98), custom_call_target="InvertDiagBlocksLowerTriangular" | custom-call | tf_op jit(solution)/shard_map/jit(cholesky)/cholesky | solution.py:243
  229.1 11.7 %cholesky.147 = f32[128,128]{1,0:T(8,128)S(1)} custom-call(f32[128,128]{1,0:T(8,128)S(1)} %convolution_subtract_fusion.3), custom_call_target="Cholesky" | custom-call | tf_op jit(solution)/shard_map/jit(cholesky)/cholesky | solution.py:243
  243.7 4.1 while.4
  247.7 19.8 %custom-call.14 = f32[2,128,128]{1,2,0:T(8,128)S(1)} custom-call(f32[2,128,128]{2,1,0:T(8,128)S(1)} %get-tuple-element.19), custom_call_target="InvertDiagBlocksLowerTriangular" | custom-call | tf_op jit(solution)/shard_map/jit(_solve_triangular)/triangular_solve | solution.py:245
  269.1 20.7 %shard_map.69 = f32[256,256]{1,0:T(8,128)S(1)} custom-call(f32[512,256]{1,0:T(8,128)S(1)} %fusion.161.left.right, f32[512,256]{1,0:T(8,128)S(1)} %fusion.161.left.right), custom_call_target="tpu_custom_call" | custom-call | tf_op jit(solution)/shard_map/pallas_call | solution.py:185
  290.0 11.7 %cholesky.164 = f32[128,128]{1,0:T(8,128)S(1)} custom-call(f32[128,128]{1,0:T(8,128)S(1)} %cholesky.197), custom_call_target="Cholesky" | custom-call | tf_op jit(solution)/shard_map/jit(cholesky)/cholesky | solution.py:243
  301.8 9.8 %custom-call.15 = f32[1,128,128]{1,2,0:T(8,128)S(1)} custom-call(f32[1,128,128]{2,1,0:T(8,128)S(1)} %get-tuple-element.94), custom_call_target="InvertDiagBlocksLowerTriangular" | custom-call | tf_op jit(solution)/shard_map/jit(cholesky)/cholesky | solution.py:243
  312.1 11.7 %cholesky.181 = f32[128,128]{1,0:T(8,128)S(1)} custom-call(f32[128,128]{1,0:T(8,128)S(1)} %convolution_subtract_fusion.2), custom_call_target="Cholesky" | custom-call | tf_op jit(solution)/shard_map/jit(cholesky)/cholesky | solution.py:243
  326.6 4.1 while.5
  330.7 19.9 %custom-call.16 = f32[2,128,128]{1,2,0:T(8,128)S(1)} custom-call(f32[2,128,128]{2,1,0:T(8,128)S(1)} %get-tuple-element.20), custom_call_target="InvertDiagBlocksLowerTriangular" | custom-call | tf_op jit(solution)/shard_map/jit(_solve_triangular)/triangular_solve | solution.py:245
  360.4 4.0 collective-permute-start.26
  367.9 4.0 collective-permute-start.29
  374.0 9.7 %fusion.31 = f32[8,8,8,256]{3,2,1,0:T(8,128)S(1)} fusion(f32[10,10,9,256]{3,2,1,0:T(8,128)S(1)} %get-tuple-element.44, f32[10,10,9,256]{3,2,1,0:T(8,128)S(1)} %get-tuple-element.43, f32[10,9,8,256]{3,2,1,0:T(8,128)S(1)} %get-tuple-element.64, f32[10,9,8,256]{3,2,1,0:T(8,128)S(1)} %get-tuple-element.63, f32[8,8,8,256]{3,2,1,0:T(8,128)S(1)} %bitcast.92, ...), kind=kLoop, calls=%fused_computation.66 | loop fusion | flops 7208960 | bytes 13764660 | tf_op jit(solution)/shard_map/add | solution.py:45
  383.7 33.2 %shard_map.70 = f32[256,256]{1,0:T(8,128)S(1)} custom-call(f32[512,256]{1,0:T(8,128)S(1)} %fusion.165.left, f32[512,256]{1,0:T(8,128)S(1)} %bitcast.97), custom_call_target="tpu_custom_call" | custom-call | tf_op jit(solution)/shard_map/pallas_call | solution.py:185
  (132 shorter events, 75.9 us)
Async XLA Ops:
  0.6 35.5 %copy-start.3 = (f32[13]{0:T(128)S(1)}, f32[13]{0:T(128)}, u32[]{:S(2)}) copy-start(f32[13]{0:T(128)} %param.9) | copy-start | bytes 160
  1.5 28.1 %collective-permute-start = (f32[1,8,8,256]{3,2,1,0:T(8,128)S(1)}, f32[1,8,8,256]{3,2,1,0:T(8,128)S(1)}, u32[]{:S(2)}, u32[]{:S(2)}) collective-permute-start(f32[1,8,8,256]{3,2,1,0:T(8,128)S(1)} %get-tuple-element.90), channel_id=1, source_target_pairs={{0,64},{64,128},{128,192},{1,65},{65,129},{129,193},{2,66},{66,130... | collective-permute-start | bytes 196616 | tf_op jit(solution)/shard_map/ppermute | solution.py:20
  6.1 24.6 %collective-permute-start.1 = (f32[1,8,8,256]{3,2,1,0:T(8,128)S(1)}, f32[1,8,8,256]{3,2,1,0:T(8,128)S(1)}, u32[]{:S(2)}, u32[]{:S(2)}) collective-permute-start(f32[1,8,8,256]{3,2,1,0:T(8,128)S(1)} %get-tuple-element.89), channel_id=1, source_target_pairs={{64,0},{128,64},{192,128},{65,1},{129,65},{193,129},{66,2},{130,66... | collective-permute-start | bytes 196616 | tf_op jit(solution)/shard_map/ppermute | solution.py:23
  30.8 7.3 %collective-permute-start.3 = (f32[10,1,8,256]{3,2,1,0:T(8,128)S(1)}, f32[10,1,8,256]{3,2,1,0:T(8,128)S(1)}, u32[]{:S(2)}, u32[]{:S(2)}) collective-permute-start(f32[10,1,8,256]{3,2,1,0:T(8,128)S(1)} %get-tuple-element.80), channel_id=1, source_target_pairs={{8,0},{16,8},{24,16},{32,24},{40,32},{48,40},{56,48},{9,1},{17,9},... | collective-permute-start | bytes 245768 | tf_op jit(solution)/shard_map/ppermute | solution.py:23
  32.1 6.0 %collective-permute-start.2 = (f32[10,1,8,256]{3,2,1,0:T(8,128)S(1)}, f32[10,1,8,256]{3,2,1,0:T(8,128)S(1)}, u32[]{:S(2)}, u32[]{:S(2)}) collective-permute-start(f32[10,1,8,256]{3,2,1,0:T(8,128)S(1)} %get-tuple-element.79), channel_id=1, source_target_pairs={{0,8},{8,16},{16,24},{24,32},{32,40},{40,48},{48,56},{1,9},{9,17},... | collective-permute-start | bytes 245768 | tf_op jit(solution)/shard_map/ppermute | solution.py:20
  38.2 6.0 %collective-permute-start.4 = (f32[10,10,1,256]{3,2,1,0:T(1,128)S(1)}, f32[10,10,1,256]{3,2,1,0:T(1,128)S(1)}, u32[]{:S(2)}, u32[]{:S(2)}) collective-permute-start(f32[10,10,1,256]{3,2,1,0:T(1,128)S(1)} %get-tuple-element.61), channel_id=1, source_target_pairs={{1,0},{2,1},{3,2},{4,3},{5,4},{6,5},{7,6},{9,8},{10,9},{11,10},{12... | collective-permute-start | bytes 307208 | tf_op jit(solution)/shard_map/ppermute | solution.py:23
  39.5 5.7 %collective-permute-start.5 = (f32[10,10,1,256]{3,2,1,0:T(1,128)S(1)}, f32[10,10,1,256]{3,2,1,0:T(1,128)S(1)}, u32[]{:S(2)}, u32[]{:S(2)}) collective-permute-start(f32[10,10,1,256]{3,2,1,0:T(1,128)S(1)} %get-tuple-element.62), channel_id=1, source_target_pairs={{0,1},{1,2},{2,3},{3,4},{4,5},{5,6},{6,7},{8,9},{9,10},{10,11},{11... | collective-permute-start | bytes 307208 | tf_op jit(solution)/shard_map/ppermute | solution.py:20
  55.5 7.4 %collective-permute-start.7 = (f32[1,8,8,256]{3,2,1,0:T(8,128)S(1)}, f32[1,8,8,256]{3,2,1,0:T(8,128)S(1)}, u32[]{:S(2)}, u32[]{:S(2)}) collective-permute-start(f32[1,8,8,256]{3,2,1,0:T(8,128)S(1)} %get-tuple-element.88), channel_id=1, source_target_pairs={{64,0},{128,64},{192,128},{65,1},{129,65},{193,129},{66,2},{130,66... | collective-permute-start | bytes 196616 | tf_op jit(solution)/shard_map/ppermute | solution.py:23
  60.5 3.8 collective-permute-start.6
  64.2 6.5 %collective-permute-start.9 = (f32[10,1,8,256]{3,2,1,0:T(8,128)S(1)}, f32[10,1,8,256]{3,2,1,0:T(8,128)S(1)}, u32[]{:S(2)}, u32[]{:S(2)}) collective-permute-start(f32[10,1,8,256]{3,2,1,0:T(8,128)S(1)} %get-tuple-element.78), channel_id=1, source_target_pairs={{8,0},{16,8},{24,16},{32,24},{40,32},{48,40},{56,48},{9,1},{17,9},... | collective-permute-start | bytes 245768 | tf_op jit(solution)/shard_map/ppermute | solution.py:23
  65.5 6.9 %collective-permute-start.8 = (f32[10,1,8,256]{3,2,1,0:T(8,128)S(1)}, f32[10,1,8,256]{3,2,1,0:T(8,128)S(1)}, u32[]{:S(2)}, u32[]{:S(2)}) collective-permute-start(f32[10,1,8,256]{3,2,1,0:T(8,128)S(1)} %get-tuple-element.77), channel_id=1, source_target_pairs={{0,8},{8,16},{16,24},{24,32},{32,40},{40,48},{48,56},{1,9},{9,17},... | collective-permute-start | bytes 245768 | tf_op jit(solution)/shard_map/ppermute | solution.py:20
  72.5 6.9 %collective-permute-start.10 = (f32[10,10,1,256]{3,2,1,0:T(1,128)S(1)}, f32[10,10,1,256]{3,2,1,0:T(1,128)S(1)}, u32[]{:S(2)}, u32[]{:S(2)}) collective-permute-start(f32[10,10,1,256]{3,2,1,0:T(1,128)S(1)} %get-tuple-element.57), channel_id=1, source_target_pairs={{1,0},{2,1},{3,2},{4,3},{5,4},{6,5},{7,6},{9,8},{10,9},{11,10},{12... | collective-permute-start | bytes 307208 | tf_op jit(solution)/shard_map/ppermute | solution.py:23
  73.8 6.5 %collective-permute-start.11 = (f32[10,10,1,256]{3,2,1,0:T(1,128)S(1)}, f32[10,10,1,256]{3,2,1,0:T(1,128)S(1)}, u32[]{:S(2)}, u32[]{:S(2)}) collective-permute-start(f32[10,10,1,256]{3,2,1,0:T(1,128)S(1)} %get-tuple-element.58), channel_id=1, source_target_pairs={{0,1},{1,2},{2,3},{3,4},{4,5},{5,6},{6,7},{8,9},{9,10},{10,11},{11... | collective-permute-start | bytes 307208 | tf_op jit(solution)/shard_map/ppermute | solution.py:20
  90.7 7.0 %collective-permute-start.13 = (f32[1,8,8,256]{3,2,1,0:T(8,128)S(1)}, f32[1,8,8,256]{3,2,1,0:T(8,128)S(1)}, u32[]{:S(2)}, u32[]{:S(2)}) collective-permute-start(f32[1,8,8,256]{3,2,1,0:T(8,128)S(1)} %get-tuple-element.86), channel_id=1, source_target_pairs={{64,0},{128,64},{192,128},{65,1},{129,65},{193,129},{66,2},{130,66... | collective-permute-start | bytes 196616 | tf_op jit(solution)/shard_map/ppermute | solution.py:23
  93.8 5.1 %collective-permute-start.12 = (f32[1,8,8,256]{3,2,1,0:T(8,128)S(1)}, f32[1,8,8,256]{3,2,1,0:T(8,128)S(1)}, u32[]{:S(2)}, u32[]{:S(2)}) collective-permute-start(f32[1,8,8,256]{3,2,1,0:T(8,128)S(1)} %get-tuple-element.85), channel_id=1, source_target_pairs={{0,64},{64,128},{128,192},{1,65},{65,129},{129,193},{2,66},{66,130... | collective-permute-start | bytes 196616 | tf_op jit(solution)/shard_map/ppermute | solution.py:20
  99.0 6.1 %collective-permute-start.15 = (f32[10,1,8,256]{3,2,1,0:T(8,128)S(1)}, f32[10,1,8,256]{3,2,1,0:T(8,128)S(1)}, u32[]{:S(2)}, u32[]{:S(2)}) collective-permute-start(f32[10,1,8,256]{3,2,1,0:T(8,128)S(1)} %get-tuple-element.74), channel_id=1, source_target_pairs={{8,0},{16,8},{24,16},{32,24},{40,32},{48,40},{56,48},{9,1},{17,9},... | collective-permute-start | bytes 245768 | tf_op jit(solution)/shard_map/ppermute | solution.py:23
  100.3 6.1 %collective-permute-start.14 = (f32[10,1,8,256]{3,2,1,0:T(8,128)S(1)}, f32[10,1,8,256]{3,2,1,0:T(8,128)S(1)}, u32[]{:S(2)}, u32[]{:S(2)}) collective-permute-start(f32[10,1,8,256]{3,2,1,0:T(8,128)S(1)} %get-tuple-element.73), channel_id=1, source_target_pairs={{0,8},{8,16},{16,24},{24,32},{32,40},{40,48},{48,56},{1,9},{9,17},... | collective-permute-start | bytes 245768 | tf_op jit(solution)/shard_map/ppermute | solution.py:20
  106.5 6.6 %collective-permute-start.16 = (f32[10,10,1,256]{3,2,1,0:T(1,128)S(1)}, f32[10,10,1,256]{3,2,1,0:T(1,128)S(1)}, u32[]{:S(2)}, u32[]{:S(2)}) collective-permute-start(f32[10,10,1,256]{3,2,1,0:T(1,128)S(1)} %get-tuple-element.53), channel_id=1, source_target_pairs={{1,0},{2,1},{3,2},{4,3},{5,4},{6,5},{7,6},{9,8},{10,9},{11,10},{12... | collective-permute-start | bytes 307208 | tf_op jit(solution)/shard_map/ppermute | solution.py:23
  107.8 7.0 %collective-permute-start.17 = (f32[10,10,1,256]{3,2,1,0:T(1,128)S(1)}, f32[10,10,1,256]{3,2,1,0:T(1,128)S(1)}, u32[]{:S(2)}, u32[]{:S(2)}) collective-permute-start(f32[10,10,1,256]{3,2,1,0:T(1,128)S(1)} %get-tuple-element.54), channel_id=1, source_target_pairs={{0,1},{1,2},{2,3},{3,4},{4,5},{5,6},{6,7},{8,9},{9,10},{10,11},{11... | collective-permute-start | bytes 307208 | tf_op jit(solution)/shard_map/ppermute | solution.py:20
  125.2 7.2 %collective-permute-start.19 = (f32[1,8,8,256]{3,2,1,0:T(8,128)S(1)}, f32[1,8,8,256]{3,2,1,0:T(8,128)S(1)}, u32[]{:S(2)}, u32[]{:S(2)}) collective-permute-start(f32[1,8,8,256]{3,2,1,0:T(8,128)S(1)} %get-tuple-element.84), channel_id=1, source_target_pairs={{64,0},{128,64},{192,128},{65,1},{129,65},{193,129},{66,2},{130,66... | collective-permute-start | bytes 196616 | tf_op jit(solution)/shard_map/ppermute | solution.py:23
  127.2 6.6 %collective-permute-start.18 = (f32[1,8,8,256]{3,2,1,0:T(8,128)S(1)}, f32[1,8,8,256]{3,2,1,0:T(8,128)S(1)}, u32[]{:S(2)}, u32[]{:S(2)}) collective-permute-start(f32[1,8,8,256]{3,2,1,0:T(8,128)S(1)} %get-tuple-element.83), channel_id=1, source_target_pairs={{0,64},{64,128},{128,192},{1,65},{65,129},{129,193},{2,66},{66,130... | collective-permute-start | bytes 196616 | tf_op jit(solution)/shard_map/ppermute | solution.py:20
  133.7 6.0 %collective-permute-start.21 = (f32[10,1,8,256]{3,2,1,0:T(8,128)S(1)}, f32[10,1,8,256]{3,2,1,0:T(8,128)S(1)}, u32[]{:S(2)}, u32[]{:S(2)}) collective-permute-start(f32[10,1,8,256]{3,2,1,0:T(8,128)S(1)} %get-tuple-element.70), channel_id=1, source_target_pairs={{8,0},{16,8},{24,16},{32,24},{40,32},{48,40},{56,48},{9,1},{17,9},... | collective-permute-start | bytes 245768 | tf_op jit(solution)/shard_map/ppermute | solution.py:23
  135.0 6.1 %collective-permute-start.20 = (f32[10,1,8,256]{3,2,1,0:T(8,128)S(1)}, f32[10,1,8,256]{3,2,1,0:T(8,128)S(1)}, u32[]{:S(2)}, u32[]{:S(2)}) collective-permute-start(f32[10,1,8,256]{3,2,1,0:T(8,128)S(1)} %get-tuple-element.69), channel_id=1, source_target_pairs={{0,8},{8,16},{16,24},{24,32},{32,40},{40,48},{48,56},{1,9},{9,17},... | collective-permute-start | bytes 245768 | tf_op jit(solution)/shard_map/ppermute | solution.py:20
  141.3 6.1 %collective-permute-start.22 = (f32[10,10,1,256]{3,2,1,0:T(1,128)S(1)}, f32[10,10,1,256]{3,2,1,0:T(1,128)S(1)}, u32[]{:S(2)}, u32[]{:S(2)}) collective-permute-start(f32[10,10,1,256]{3,2,1,0:T(1,128)S(1)} %get-tuple-element.49), channel_id=1, source_target_pairs={{1,0},{2,1},{3,2},{4,3},{5,4},{6,5},{7,6},{9,8},{10,9},{11,10},{12... | collective-permute-start | bytes 307208 | tf_op jit(solution)/shard_map/ppermute | solution.py:23
  142.6 6.3 %collective-permute-start.23 = (f32[10,10,1,256]{3,2,1,0:T(1,128)S(1)}, f32[10,10,1,256]{3,2,1,0:T(1,128)S(1)}, u32[]{:S(2)}, u32[]{:S(2)}) collective-permute-start(f32[10,10,1,256]{3,2,1,0:T(1,128)S(1)} %get-tuple-element.50), channel_id=1, source_target_pairs={{0,1},{1,2},{2,3},{3,4},{4,5},{5,6},{6,7},{8,9},{9,10},{10,11},{11... | collective-permute-start | bytes 307208 | tf_op jit(solution)/shard_map/ppermute | solution.py:20
  352.1 31.5 %copy-start = (f32[512,256]{1,0:T(8,128)}, f32[512,256]{1,0:T(8,128)S(1)}, u32[]{:S(2)}) copy-start(f32[512,256]{1,0:T(8,128)S(1)} %fusion.165.left) | copy-start | bytes 1572868
  352.2 5.6 %collective-permute-start.25 = (f32[1,8,8,256]{3,2,1,0:T(8,128)S(1)}, f32[1,8,8,256]{3,2,1,0:T(8,128)S(1)}, u32[]{:S(2)}, u32[]{:S(2)}) collective-permute-start(f32[1,8,8,256]{3,2,1,0:T(8,128)S(1)} %get-tuple-element.82), channel_id=1, source_target_pairs={{64,0},{128,64},{192,128},{65,1},{129,65},{193,129},{66,2},{130,66... | collective-permute-start | bytes 196616 | tf_op jit(solution)/shard_map/ppermute | solution.py:23
  354.8 4.2 %collective-permute-start.24 = (f32[1,8,8,256]{3,2,1,0:T(8,128)S(1)}, f32[1,8,8,256]{3,2,1,0:T(8,128)S(1)}, u32[]{:S(2)}, u32[]{:S(2)}) collective-permute-start(f32[1,8,8,256]{3,2,1,0:T(8,128)S(1)} %get-tuple-element.81), channel_id=1, source_target_pairs={{0,64},{64,128},{128,192},{1,65},{65,129},{129,193},{2,66},{66,130... | collective-permute-start | bytes 196616 | tf_op jit(solution)/shard_map/ppermute | solution.py:20
  359.1 5.6 %collective-permute-start.27 = (f32[10,1,8,256]{3,2,1,0:T(8,128)S(1)}, f32[10,1,8,256]{3,2,1,0:T(8,128)S(1)}, u32[]{:S(2)}, u32[]{:S(2)}) collective-permute-start(f32[10,1,8,256]{3,2,1,0:T(8,128)S(1)} %get-tuple-element.66), channel_id=1, source_target_pairs={{8,0},{16,8},{24,16},{32,24},{40,32},{48,40},{56,48},{9,1},{17,9},... | collective-permute-start | bytes 245768 | tf_op jit(solution)/shard_map/ppermute | solution.py:23
  360.4 6.1 %collective-permute-start.26 = (f32[10,1,8,256]{3,2,1,0:T(8,128)S(1)}, f32[10,1,8,256]{3,2,1,0:T(8,128)S(1)}, u32[]{:S(2)}, u32[]{:S(2)}) collective-permute-start(f32[10,1,8,256]{3,2,1,0:T(8,128)S(1)} %get-tuple-element.65), channel_id=1, source_target_pairs={{0,8},{8,16},{16,24},{24,32},{32,40},{40,48},{48,56},{1,9},{9,17},... | collective-permute-start | bytes 245768 | tf_op jit(solution)/shard_map/ppermute | solution.py:20
  366.6 6.2 %collective-permute-start.28 = (f32[10,10,1,256]{3,2,1,0:T(1,128)S(1)}, f32[10,10,1,256]{3,2,1,0:T(1,128)S(1)}, u32[]{:S(2)}, u32[]{:S(2)}) collective-permute-start(f32[10,10,1,256]{3,2,1,0:T(1,128)S(1)} %get-tuple-element.45), channel_id=1, source_target_pairs={{1,0},{2,1},{3,2},{4,3},{5,4},{6,5},{7,6},{9,8},{10,9},{11,10},{12... | collective-permute-start | bytes 307208 | tf_op jit(solution)/shard_map/ppermute | solution.py:23
  367.9 5.7 %collective-permute-start.29 = (f32[10,10,1,256]{3,2,1,0:T(1,128)S(1)}, f32[10,10,1,256]{3,2,1,0:T(1,128)S(1)}, u32[]{:S(2)}, u32[]{:S(2)}) collective-permute-start(f32[10,10,1,256]{3,2,1,0:T(1,128)S(1)} %get-tuple-element.46), channel_id=1, source_target_pairs={{0,1},{1,2},{2,3},{3,4},{4,5},{5,6},{6,7},{8,9},{9,10},{10,11},{11... | collective-permute-start | bytes 307208 | tf_op jit(solution)/shard_map/ppermute | solution.py:20
  (2 other events, 2.9 us)

commit v2 on v1

v2 whole, which is shorter than its diff:
```python
import functools

import jax
import jax.numpy as jnp
from jax import lax
from jax.experimental import pallas as pl
from jax.experimental.pallas import tpu as pltpu
from jax.sharding import PartitionSpec as P

DEG = 4
MESH = pl.DeviceIdType.MESH
HIGHEST = lax.Precision.HIGHEST
AXES = ("gx", "gy", "gz")
OFFSETS = [
    (dx, dy, dz)
    for dx in (-1, 0, 1)
    for dy in (-1, 0, 1)
    for dz in (-1, 0, 1)
    if (dx, dy, dz) != (0, 0, 0)
]
POSITIVE = [offset for offset in OFFSETS if offset > (0, 0, 0)]


def hop_index(offset):
    return POSITIVE.index(max(offset, tuple(-d for d in offset)))


def plane_peer(dims, offset):
    size_x, _, size_z = dims
    place = lax.axis_index("gx") * size_z + lax.axis_index("gz")
    peer = lax.rem(place + offset, size_x * size_z)
    return peer, {"gx": peer // size_z, "gz": lax.rem(peer, size_z)}


def column_peer(dims, offset):
    peer = lax.rem(lax.axis_index("gy") + offset, dims[1])
    return peer, {"gy": peer}


def has_neighbour(dims, offset):
    valid = None
    for axis, size, step in zip(AXES, dims, offset):
        if step:
            place = lax.axis_index(axis)
            here = place < size - 1 if step > 0 else place > 0
            valid = here if valid is None else jnp.logical_and(valid, here)
    return valid


def neighbour(offset):
    return {axis: lax.axis_index(axis) + step for axis, step in zip(AXES, offset) if step}


def enter(dims, halo):
    barrier = pltpu.get_barrier_semaphore()

    @pl.loop(1, dims[0] * dims[2])
    def _(k):
        pl.semaphore_signal(barrier, inc=1, device_id=plane_peer(dims, k)[1], device_id_type=MESH)

    @pl.loop(1, dims[1])
    def _(k):
        pl.semaphore_signal(barrier, inc=1, device_id=column_peer(dims, k)[1], device_id_type=MESH)

    if halo:
        for offset in OFFSETS:

            @pl.when(has_neighbour(dims, offset))
            def _():
                pl.semaphore_signal(
                    barrier, inc=1, device_id=neighbour(offset), device_id_type=MESH
                )


def entered(dims, halo):
    count = dims[0] * dims[2] + dims[1] - 2
    if halo:
        boxes = 1
        for axis, size in zip(AXES, dims):
            place = lax.axis_index(axis)
            boxes = boxes * (3 - (place == 0).astype(jnp.int32) - (place == size - 1).astype(jnp.int32))
        count = count + boxes - 1
    pl.semaphore_wait(pltpu.get_barrier_semaphore(), count)


def wait_bytes(ref, sem):
    pltpu.make_async_copy(ref, ref, sem).wait()


def send(src, dst, send_sem, recv_sem, device):
    pltpu.make_async_remote_copy(
        src_ref=src,
        dst_ref=dst,
        send_sem=send_sem,
        recv_sem=recv_sem,
        device_id=device,
        device_id_type=MESH,
    ).start()


def all_reduce(dims, local, total, plane_buf, column_buf, sems):
    plane, column = dims[0] * dims[2], dims[1]
    rows = local.shape[0] // plane
    place = lax.axis_index("gx") * dims[2] + lax.axis_index("gz")
    level = lax.axis_index("gy")
    mine = pl.ds(pl.multiple_of(place * rows, rows), rows)

    @pl.loop(1, plane)
    def _(k):
        peer, device = plane_peer(dims, k)
        theirs = pl.ds(pl.multiple_of(peer * rows, rows), rows)
        send(local.at[theirs], plane_buf.at[k - 1], sems.at[0], sems.at[1], device)

    wait_bytes(plane_buf, sems.at[1])
    column_buf[level] = lax.fori_loop(
        0, plane - 1, lambda k, acc: acc + plane_buf[k], local[mine]
    )

    @pl.loop(1, column)
    def _(k):
        _, device = column_peer(dims, k)
        send(column_buf.at[level], column_buf.at[level], sems.at[2], sems.at[3], device)

    wait_bytes(column_buf.at[pl.ds(0, column - 1)], sems.at[3])
    part = column_buf[0]
    for k in range(1, column):
        part = part + column_buf[k]
    total[mine] = part

    @pl.loop(1, plane)
    def _(k):
        _, device = plane_peer(dims, k)
        send(total.at[mine], total.at[mine], sems.at[4], sems.at[5], device)

    wait_bytes(total.at[pl.ds(0, (plane - 1) * rows)], sems.at[5])
    wait_bytes(plane_buf, sems.at[0])
    wait_bytes(column_buf.at[pl.ds(0, column - 1)], sems.at[2])
    wait_bytes(total.at[pl.ds(0, (plane - 1) * rows)], sems.at[4])


def reduce_scratch(dims, size):
    plane, column = dims[0] * dims[2], dims[1]
    rows = size // plane
    return [
        pltpu.VMEM((size, size), jnp.float32),
        pltpu.VMEM((size, size), jnp.float32),
        pltpu.VMEM((plane - 1, rows, size), jnp.float32),
        pltpu.VMEM((column, rows, size), jnp.float32),
        pltpu.SemaphoreType.DMA((6,)),
    ]


def max_start(dims, value, plane_buf, sems):
    plane = dims[0] * dims[2]
    place = lax.axis_index("gx") * dims[2] + lax.axis_index("gz")

    @pl.loop(1, plane)
    def _(k):
        _, device = plane_peer(dims, k)
        send(plane_buf.at[place], plane_buf.at[place], sems.at[0], sems.at[1], device)


def max_middle(dims, plane_buf, column_buf, sems):
    plane, column = dims[0] * dims[2], dims[1]
    level = lax.axis_index("gy")
    wait_bytes(plane_buf.at[pl.ds(0, plane - 1)], sems.at[1])
    column_buf[level] = jnp.max(plane_buf[...], axis=0)

    @pl.loop(1, column)
    def _(k):
        _, device = column_peer(dims, k)
        send(column_buf.at[level], column_buf.at[level], sems.at[2], sems.at[3], device)


def max_end(dims, plane_buf, column_buf, sems):
    plane, column = dims[0] * dims[2], dims[1]
    wait_bytes(column_buf.at[pl.ds(0, column - 1)], sems.at[3])
    wait_bytes(plane_buf.at[pl.ds(0, plane - 1)], sems.at[0])
    wait_bytes(column_buf.at[pl.ds(0, column - 1)], sems.at[2])
    return jnp.max(column_buf[...], axis=0)


def halo_scratch(shape, slots):
    size_x, size_y, size_z, columns = shape
    f32 = jnp.float32
    return [
        pltpu.VMEM((slots, size_x + 2, size_y + 2, size_z, columns), f32),
        pltpu.VMEM((slots, 2, size_x + 2, size_y, columns), f32),
        pltpu.VMEM((slots, 2, 2, size_x, columns), f32),
        pltpu.VMEM((slots, 2, 2, 2, 8, columns), f32),
        pltpu.VMEM((slots, 2, size_x, size_y, columns), f32),
        pltpu.VMEM((slots, 2, 2, size_x, columns), f32),
        pltpu.VMEM((slots, 2, 2, 2, 8, columns), f32),
        pltpu.VMEM((2, size_x + 2, size_y + 2, size_z, columns), f32),
        pltpu.SemaphoreType.DMA((slots, 2, len(OFFSETS))),
    ]


def halo_parts(shape, slot, offset, field, face, edge, corner, face_out, edge_out, corner_out):
    size_x, size_y, _, _ = shape
    sx, sy, sz = offset
    low = {1: 0, -1: 1}

    def ends(step, size):
        if step == 0:
            return pl.ds(1, size), pl.ds(1, size)
        return (size, 0) if step > 0 else (1, size + 1)

    from_x, to_x = ends(sx, size_x)
    from_y, to_y = ends(sy, size_y)
    if sz == 0:
        return field.at[slot, from_x, from_y], field.at[slot, to_x, to_y]
    top = 1 if sz > 0 else 0
    if sy == 0:
        source = pl.ds(0, size_x) if sx == 0 else from_x - 1
        return face_out.at[slot, top, source], face.at[slot, 1 - top, to_x]
    far = 1 if sy > 0 else 0
    if sx == 0:
        return edge_out.at[slot, top, far], edge.at[slot, 1 - top, 1 - far]
    right = 1 if sx > 0 else 0
    return (
        corner_out.at[slot, top, far, right],
        corner.at[slot, 1 - top, 1 - far, 1 - right],
    )


def zero_border(dims, shape, slots, field, face, edge, corner):
    size_x, size_y, size_z, columns = shape
    for slot in range(slots):
        for side in (0, 1):
            step = 1 if side else -1
            row = size_x + 1 if side else 0

            @pl.when(jnp.logical_not(has_neighbour(dims, (step, 0, 0))))
            def _():
                field[slot, row] = jnp.zeros((size_y + 2, size_z, columns), jnp.float32)
                for top in (0, 1):
                    face[slot, top, row] = jnp.zeros((size_y, columns), jnp.float32)
                    for far in (0, 1):
                        corner[slot, top, far, side] = jnp.zeros((8, columns), jnp.float32)

            row_y = size_y + 1 if side else 0

            @pl.when(jnp.logical_not(has_neighbour(dims, (0, step, 0))))
            def _():
                field[slot, :, row_y] = jnp.zeros((size_x + 2, size_z, columns), jnp.float32)
                for top in (0, 1):
                    edge[slot, top, side] = jnp.zeros((size_x, columns), jnp.float32)
                    for right in (0, 1):
                        corner[slot, top, side, right] = jnp.zeros((8, columns), jnp.float32)

            @pl.when(jnp.logical_not(has_neighbour(dims, (0, 0, step))))
            def _():
                face[slot, side] = jnp.zeros((size_x + 2, size_y, columns), jnp.float32)
                edge[slot, side] = jnp.zeros((2, size_x, columns), jnp.float32)
                corner[slot, side] = jnp.zeros((2, 2, 8, columns), jnp.float32)


def pack_column(shape, slot, x, y, value, face_out, edge_out):
    size_y, size_z = shape[1], shape[2]
    for top, z in ((0, 0), (1, size_z - 1)):
        row = value[z : z + 1]
        face_out[slot, top, x, y : y + 1] = row
        if y in (0, size_y - 1):
            edge_out[slot, top, 1 if y else 0, pl.ds(x, 1)] = row


def pack_corners(shape, slot, field, corner_out):
    size_x, size_y, size_z, columns = shape
    for top in (0, 1):
        for far in (0, 1):
            for right in (0, 1):
                z = (size_z - 1) * top
                corner_out[slot, top, far, right] = jnp.broadcast_to(
                    field[slot, size_x if right else 1, size_y if far else 1, z : z + 1],
                    (8, columns),
                )


def halo_send(dims, shape, slot, refs, sems):
    for index, offset in enumerate(OFFSETS):

        @pl.when(has_neighbour(dims, offset))
        def _():
            src, dst = halo_parts(shape, slot, offset, *refs)
            send(src, dst, sems.at[slot, 0, index], sems.at[slot, 1, index], neighbour(offset))


def halo_wait(dims, shape, slot, refs, sems, received):
    for index, offset in enumerate(OFFSETS):
        from_there = tuple(-step for step in offset)

        @pl.when(has_neighbour(dims, from_there if received else offset))
        def _():
            src, dst = halo_parts(shape, slot, offset, *refs)
            if received:
                wait_bytes(dst, sems.at[slot, 1, index])
            else:
                wait_bytes(src, sems.at[slot, 0, index])


def shift_columns(shape, slot, field, face, edge, corner, shifted):
    size_x, size_y, size_z, columns = shape
    place = lax.broadcasted_iota(jnp.int32, (size_z, columns), 0)

    def put(x, y, below, above):
        value = field[slot, x, y]
        shifted[0, x, y] = jnp.where(place == 0, below, pltpu.roll(value, 1, 0))
        shifted[1, x, y] = jnp.where(place == size_z - 1, above, pltpu.roll(value, size_z - 1, 0))

    @pl.loop(0, size_x + 2)
    def _(x):
        for y in range(size_y):
            put(x, y + 1, face[slot, 0, x, y : y + 1], face[slot, 1, x, y : y + 1])

    for far in (0, 1):
        y = size_y + 1 if far else 0

        @pl.loop(0, size_x)
        def _(x):
            put(x + 1, y, edge[slot, 0, far, pl.ds(x, 1)], edge[slot, 1, far, pl.ds(x, 1)])

        for right in (0, 1):
            x = size_x + 1 if right else 0
            put(x, y, corner[slot, 0, far, right], corner[slot, 1, far, right])


def apply_rows(shape, slot, x, field, shifted, onsite, hopping):
    size_y, columns = shape[1], shape[3]
    totals = [None] * size_y
    centres = [None] * size_y
    for dx in (-1, 0, 1):
        for y in range(-1, size_y + 1):
            for dz in (-1, 0, 1):
                if dz == 0:
                    value = field[slot, x + 1 + dx, y + 1]
                else:
                    value = shifted[0 if dz < 0 else 1, x + 1 + dx, y + 1]
                for dy in (-1, 0, 1):
                    target = y - dy
                    if not 0 <= target < size_y:
                        continue
                    if (dx, dy, dz) == (0, 0, 0):
                        centres[target] = value
                        level = onsite[x, target]
                        term = jnp.concatenate([level] * (columns // level.shape[1]), 1) * value
                    else:
                        term = hopping[hop_index((dx, dy, dz))] * value
                    totals[target] = term if totals[target] is None else totals[target] + term
    return totals, centres


def filter_kernel(
    dims, shape, sites,
    block, onsite, hopping, cut_frac,
    flat, gram,
    field, face, edge, corner, face_out, edge_out, corner_out, shifted, halo_sems,
    max_plane, max_column, max_sems, coef,
    local, total, plane_buf, column_buf, sums_sems,
):
    size_x, size_y, size_z, columns = shape
    refs = (field, face, edge, corner, face_out, edge_out, corner_out)
    zero_border(dims, shape, 2, field, face, edge, corner)
    enter(dims, True)
    place = lax.axis_index("gx") * dims[2] + lax.axis_index("gz")
    max_plane[place] = jnp.full((8, 128), jnp.max(jnp.abs(onsite[...])), jnp.float32)

    @pl.loop(0, size_x)
    def _(x):
        for y in range(size_y):
            value = block[x, y]
            field[0, x + 1, y + 1] = value
            pack_column(shape, 0, x, y, value, face_out, edge_out)

    pack_corners(shape, 0, field, corner_out)
    entered(dims, True)
    for step in range(DEG):
        slot, after = step % 2, (step + 1) % 2
        halo_send(dims, shape, slot, refs, halo_sems)
        if step == 0:
            max_start(dims, None, max_plane, max_sems)
            max_middle(dims, max_plane, max_column, max_sems)
        halo_wait(dims, shape, slot, refs, halo_sems, True)
        shift_columns(shape, slot, field, face, edge, corner, shifted)
        if step == 0:
            bound = max_end(dims, max_plane, max_column, max_sems)
            reach = jnp.abs(hopping[0])
            for k in range(1, len(POSITIVE)):
                reach = reach + jnp.abs(hopping[k])
            bound = bound + 2.0 * reach
            cut = cut_frac[0] * bound
            half_width = (bound - cut) / 2.0
            center = (bound + cut) / 2.0
            sigma_one = half_width / (-bound - center)
            sigma = sigma_one
            coef[0] = center
            coef[1] = sigma / half_width
            for k in range(1, DEG):
                sigma_next = 1.0 / (2.0 / sigma_one - sigma)
                coef[2 * k] = 2.0 * sigma_next / half_width
                coef[2 * k + 1] = sigma * sigma_next
                sigma = sigma_next
        if step:
            halo_wait(dims, shape, after, refs, halo_sems, False)

        @pl.loop(0, size_x)
        def _(x):
            wide = lambda k: jnp.concatenate([coef[k]] * (columns // 128), 1)
            totals, centres = apply_rows(shape, slot, x, field, shifted, onsite, hopping)
            for y in range(size_y):
                value = totals[y] - wide(0) * centres[y]
                if step == 0:
                    value = wide(1) * value
                else:
                    older = field[after, x + 1, y + 1]
                    value = wide(2 * step) * value - wide(2 * step + 1) * older
                if step == DEG - 1:
                    flat[pl.ds(pl.multiple_of((x * size_y + y) * size_z, size_z), size_z)] = value
                else:
                    field[after, x + 1, y + 1] = value
                    pack_column(shape, after, x, y, value, face_out, edge_out)

        if step < DEG - 1:
            pack_corners(shape, after, field, corner_out)
    halo_wait(dims, shape, (DEG - 1) % 2, refs, halo_sems, False)
    local[...] = product(flat[...], flat[...])
    all_reduce(dims, local, total, plane_buf, column_buf, sums_sems)
    gram[...] = total[...] / sites


def product(left, right):
    return lax.dot_general(
        left,
        right,
        (((0,), (0,)), ((), ())),
        precision=HIGHEST,
        preferred_element_type=jnp.float32,
    )


def rotated(flat, factor):
    return lax.dot_general(
        flat,
        factor,
        (((1,), (1,)), ((), ())),
        precision=HIGHEST,
        preferred_element_type=jnp.float32,
    )


def rotate_kernel(
    dims, sites, flat, factor, first, gram, local, total, plane_buf, column_buf, sums_sems
):
    enter(dims, False)
    first[...] = rotated(flat[...], factor[...])
    local[...] = product(first[...], first[...])
    entered(dims, False)
    all_reduce(dims, local, total, plane_buf, column_buf, sums_sems)
    gram[...] = total[...] / sites


def project_kernel(
    dims, shape, sites,
    first, factor, onsite, hopping,
    states, gram,
    field, face, edge, corner, face_out, edge_out, corner_out, shifted, halo_sems, image,
    local, total, plane_buf, column_buf, sums_sems,
):
    size_x, size_y, size_z, columns = shape
    refs = (field, face, edge, corner, face_out, edge_out, corner_out)
    zero_border(dims, shape, 1, field, face, edge, corner)
    enter(dims, True)
    states[...] = rotated(first[...], factor[...])

    def rows(x, y):
        return pl.ds(pl.multiple_of((x * size_y + y) * size_z, size_z), size_z)

    @pl.loop(0, size_x)
    def _(x):
        for y in range(size_y):
            value = states[rows(x, y)]
            field[0, x + 1, y + 1] = value
            pack_column(shape, 0, x, y, value, face_out, edge_out)

    pack_corners(shape, 0, field, corner_out)
    entered(dims, True)
    halo_send(dims, shape, 0, refs, halo_sems)
    halo_wait(dims, shape, 0, refs, halo_sems, True)
    shift_columns(shape, 0, field, face, edge, corner, shifted)

    @pl.loop(0, size_x)
    def _(x):
        totals, _ = apply_rows(shape, 0, x, field, shifted, onsite, hopping)
        for y in range(size_y):
            image[rows(x, y)] = totals[y]

    halo_wait(dims, shape, 0, refs, halo_sems, False)
    local[...] = product(states[...], image[...])
    all_reduce(dims, local, total, plane_buf, column_buf, sums_sems)
    gram[...] = total[...] / sites


def call(kernel, inputs, scalars, outputs, scratch, ident):
    vmem = pl.BlockSpec(memory_space=pltpu.VMEM)
    smem = pl.BlockSpec(memory_space=pltpu.SMEM)
    return pl.pallas_call(
        kernel,
        out_shape=[jax.ShapeDtypeStruct(shape, jnp.float32) for shape in outputs],
        in_specs=[vmem] * len(inputs) + [smem] * len(scalars),
        out_specs=[vmem] * len(outputs),
        scratch_shapes=scratch,
        compiler_params=pltpu.CompilerParams(
            collective_id=ident, has_side_effects=True, vmem_limit_bytes=48 << 20
        ),
    )(*inputs, *scalars)


def lower_and_inverse(gram):
    lower = jnp.linalg.cholesky(gram)
    ident = jnp.eye(gram.shape[0], dtype=jnp.float32)
    return (lower, jax.scipy.linalg.solve_triangular(lower, ident, lower=True))


def body(dims, block, onsite, hopping, cut_frac):
    shape = block.shape
    size_x, size_y, size_z, columns = shape
    count = size_x * size_y * size_z
    sites = count * dims[0] * dims[1] * dims[2]
    plane, column = dims[0] * dims[2], dims[1]
    sums = reduce_scratch(dims, columns)
    levels = jnp.broadcast_to(onsite[..., None], onsite.shape + (128,))
    flat, gram_one = call(
        functools.partial(filter_kernel, dims, shape, sites),
        [block, levels],
        [hopping, cut_frac],
        [(count, columns), (columns, columns)],
        halo_scratch(shape, 2)
        + [
            pltpu.VMEM((plane, 8, 128), jnp.float32),
            pltpu.VMEM((column, 8, 128), jnp.float32),
            pltpu.SemaphoreType.DMA((4,)),
            pltpu.VMEM((2 * DEG, 8, 128), jnp.float32),
        ]
        + sums,
        1,
    )
    lower_one, inverse_one = lower_and_inverse(gram_one)
    first, gram_two = call(
        functools.partial(rotate_kernel, dims, sites),
        [flat, inverse_one],
        [],
        [(count, columns), (columns, columns)],
        sums,
        2,
    )
    _, inverse_two = lower_and_inverse(gram_two)
    states, projected = call(
        functools.partial(project_kernel, dims, shape, sites),
        [first, inverse_two, levels],
        [hopping],
        [(count, columns), (columns, columns)],
        halo_scratch(shape, 1) + [pltpu.VMEM((count, columns), jnp.float32)] + sums,
        3,
    )
    return (states.reshape(shape), projected, lower_one)


def solution(mesh):
    dims = (mesh.shape["gx"], mesh.shape["gy"], mesh.shape["gz"])
    return jax.shard_map(
        functools.partial(body, dims),
        mesh=mesh,
        in_specs=(P("gx", "gy", "gz", None), P("gx", "gy", "gz"), P(), P()),
        out_specs=(P("gx", "gy", "gz", None), P(), P()),
        check_vma=False,
    )
```

time: 426 us -> 250 us (0.59); the launches traced: 418 us -> 250 us
  starting transfers between devices: 90.5 us -> 0 us
  other arithmetic: 162 us -> 109 us
  waiting for transfers between devices: 20 us -> 0 us
    ppermute x30 -> x0, starting transfers between devices: 90.5 us -> none  [the longest x15 62.9 us: extended(): lax.ppermute(lax.slice_in_dim(block, block.shape[dim] - width, None, axis...]
    sub x3 -> x0, other arithmetic: 29.6 us -> none  [cheb_filter(): 2.0 * sigma_next / half_width * (operate(newer) - center * newer)]
    ppermute x30 -> x0, waiting for transfers between devices: 20 us -> none  [the longest x15 17.2 us: extended(): lax.ppermute(lax.slice_in_dim(block, block.shape[dim] - width, None, axis...]
    mul x1 -> x0, other arithmetic: 9.78 us -> none  [cheb_filter(): newer = sigma / half_width * (operate(older) - center * older)]
    add x1 -> x0, other arithmetic: 9.68 us -> none  [stencil(): total + hopping[index] * padded[ax_x:ax_x + size_x, ax_y:ax_y + size_y, a...]
    pallas_call x4 -> x3, Pallas kernels: 121 us -> 122 us  [call(): pl.pallas_call(kernel, out_shape=[jax.ShapeDtypeStruct(shape, jnp.float32...]
    another operation x5 -> x7, other arithmetic: 40.5 us -> 40.6 us  [lower_and_inverse(): return (lower, jax.scipy.linalg.solve_triangular(lower, ident, lower=True))]
  transfers between devices with their start and end apart: 30 -> 0, of which waited for: 18 -> 0; matrix products, arithmetic and copies ran while one was open for 1% -> 0% of each run, Pallas kernels for 5% -> 0%
where the time goes in v2:
time: 250 us
  Pallas kernels  122 us (49%)
  other arithmetic  109 us (44%)
  local copies, waits for them, and re-layouts  11.9 us (5%)
  between operations  4.21 us (2%)
  matrix products  2.7 us (1%)
    pallas_call x3, Pallas kernels, call(): pl.pallas_call(kernel, out_shape=[jax.ShapeDtypeStruct(shape, jnp.float32...  122 us
    another operation x13, other arithmetic, lower_and_inverse(): lower = jnp.linalg.cholesky(gram)  68.6 us
    another operation x7, other arithmetic, lower_and_inverse(): return (lower, jax.scipy.linalg.solve_triangular(lower, ident, lower=True))  40.6 us
    another operation x15, local copies, waits for them, and re-layouts, lower_and_inverse(): return (lower, jax.scipy.linalg.solve_triangular(lower, ident, lower=True))  8.17 us

profile of v2, /device:TPU:1, one launch (start us, length us, event | category | flops | bytes accessed | tf_op | source)
XLA Modules:
  0.0 250.0 jit_solution(14786979849299742417)
XLA Ops:
  0.6 0.9 broadcast_in_dim.2.onsite
  2.2 1.0 copy-done
  3.2 68.8 %shard_map.67 = (f32[512,256]{1,0:T(8,128)S(1)}, f32[256,256]{1,0:T(8,128)S(1)}) custom-call(f32[8,8,8,256]{3,2,1,0:T(8,128)S(1)} %copy-done, f32[8,8,8,128]{3,2,1,0:T(8,128)S(1)} %broadcast_in_dim.2.onsite, f32[13]{0:T(128)S(1)} %copy-done.1, f32[1]{0:T(128)S(6)} %copy.32.cut_frac), custom_call_target="tpu_custom_call" | custom-call | tf_op jit(solution)/shard_map/pallas_call | solution.py:506
  72.2 11.7 %cholesky.130 = f32[128,128]{1,0:T(8,128)S(1)} custom-call(f32[128,128]{1,0:T(8,128)S(1)} %cholesky.194), custom_call_target="Cholesky" | custom-call | tf_op jit(solution)/shard_map/jit(cholesky)/cholesky | solution.py:519
  84.0 9.8 %custom-call.13 = f32[1,128,128]{1,2,0:T(8,128)S(1)} custom-call(f32[1,128,128]{2,1,0:T(8,128)S(1)} %get-tuple-element.62), custom_call_target="InvertDiagBlocksLowerTriangular" | custom-call | tf_op jit(solution)/shard_map/jit(cholesky)/cholesky | solution.py:519
  94.3 11.7 %cholesky.147 = f32[128,128]{1,0:T(8,128)S(1)} custom-call(f32[128,128]{1,0:T(8,128)S(1)} %convolution_subtract_fusion.3), custom_call_target="Cholesky" | custom-call | tf_op jit(solution)/shard_map/jit(cholesky)/cholesky | solution.py:519
  106.1 0.6 compare_reduce_fusion.2
  108.0 0.7 fusion.3
  108.8 4.1 %while.4 = (s32[]{:T(128)}, f32[256,256]{1,0:T(8,128)S(1)}, s32[2,2]{1,0:T(2,128)S(1)}, f32[2,128,128]{2,1,0:T(8,128)S(1)}, s32[]{:T(128)}) while((s32[]{:T(128)}, f32[256,256]{1,0:T(8,128)S(1)}, s32[2,2]{1,0:T(2,128)S(1)}, f32[2,128,128]{2,1,0:T(8,128)S(1)}, s32[]{:T(128)}) %tuple.48), condition=%wide.while_cond, body=%wide.while_body.sunk | while | flops 2 | bytes 131181 | solution.py:521
  108.9 0.7 fusion.32
  109.5 1.3 bitcast_dynamic-update-slice_fusion.4
  110.9 0.7 fusion.32
  111.6 1.3 bitcast_dynamic-update-slice_fusion.4
  112.9 19.9 %custom-call.14 = f32[2,128,128]{1,2,0:T(8,128)S(1)} custom-call(f32[2,128,128]{2,1,0:T(8,128)S(1)} %get-tuple-element.31), custom_call_target="InvertDiagBlocksLowerTriangular" | custom-call | tf_op jit(solution)/shard_map/jit(_solve_triangular)/triangular_solve | solution.py:521
  132.9 0.3 fusion.7
  133.4 0.3 fusion.14
  133.8 20.7 %shard_map.68 = (f32[512,256]{1,0:T(8,128)S(1)}, f32[256,256]{1,0:T(8,128)S(1)}) custom-call(f32[512,256]{1,0:T(8,128)S(1)} %get-tuple-element.11.flat, f32[256,256]{1,0:T(8,128)S(1)} %pad_maximum_fusion.factor), custom_call_target="tpu_custom_call" | custom-call | tf_op jit(solution)/shard_map/pallas_call | solution.py:506
  154.7 11.7 %cholesky.164 = f32[128,128]{1,0:T(8,128)S(1)} custom-call(f32[128,128]{1,0:T(8,128)S(1)} %cholesky.197), custom_call_target="Cholesky" | custom-call | tf_op jit(solution)/shard_map/jit(cholesky)/cholesky | solution.py:519
  166.4 9.8 %custom-call.15 = f32[1,128,128]{1,2,0:T(8,128)S(1)} custom-call(f32[1,128,128]{2,1,0:T(8,128)S(1)} %get-tuple-element.58), custom_call_target="InvertDiagBlocksLowerTriangular" | custom-call | tf_op jit(solution)/shard_map/jit(cholesky)/cholesky | solution.py:519
  176.7 11.7 %cholesky.181 = f32[128,128]{1,0:T(8,128)S(1)} custom-call(f32[128,128]{1,0:T(8,128)S(1)} %convolution_subtract_fusion.2), custom_call_target="Cholesky" | custom-call | tf_op jit(solution)/shard_map/jit(cholesky)/cholesky | solution.py:519
  188.5 0.7 compare_reduce_fusion
  189.2 0.6 compare_reduce_fusion.1
  191.2 4.1 %while.5 = (s32[]{:T(128)}, f32[256,256]{1,0:T(8,128)S(1)}, s32[2,2]{1,0:T(2,128)S(1)}, f32[2,128,128]{2,1,0:T(8,128)S(1)}, s32[]{:T(128)}) while((s32[]{:T(128)}, f32[256,256]{1,0:T(8,128)S(1)}, s32[2,2]{1,0:T(2,128)S(1)}, f32[2,128,128]{2,1,0:T(8,128)S(1)}, s32[]{:T(128)}) %tuple.56), condition=%wide.while_cond.clone, body=%wide.while_body.clone.sunk | while | flops 2 | bytes 131181 | solution.py:521
  191.3 0.6 fusion.33
  191.9 1.4 bitcast_dynamic-update-slice_fusion.5
  193.3 0.6 fusion.33
  193.9 1.4 bitcast_dynamic-update-slice_fusion.5
  195.4 19.9 %custom-call.16 = f32[2,128,128]{1,2,0:T(8,128)S(1)} custom-call(f32[2,128,128]{2,1,0:T(8,128)S(1)} %get-tuple-element.32), custom_call_target="InvertDiagBlocksLowerTriangular" | custom-call | tf_op jit(solution)/shard_map/jit(_solve_triangular)/triangular_solve | solution.py:521
  215.3 0.3 fusion.5
  216.2 32.2 %shard_map.69 = (f32[512,256]{1,0:T(8,128)S(1)}, f32[256,256]{1,0:T(8,128)S(1)}) custom-call(f32[512,256]{1,0:T(8,128)S(1)} %get-tuple-element.13.first, f32[256,256]{1,0:T(8,128)S(1)} %pad_maximum_fusion.1.factor, f32[8,8,8,128]{3,2,1,0:T(8,128)S(1)} %broadcast_in_dim.2.onsite, f32[13]{0:T(128)S(1)} %copy-done.1), custom_call_target="tpu_custom_call" | custom-call | tf_op jit(solution)/shard_map/pallas_call | solution.py:506
  248.5 0.8 copy.34
  249.3 0.7 copy.35
  (34 shorter events, 2.5 us)
Async XLA Ops:
  1.5 0.7 copy-start.1
  2.2 1.0 copy-start

commit v3 on v2

--- a/solution.py
+++ b/solution.py
@@ -515,10 +515,101 @@
     )(*inputs, *scalars)
 
 
-def lower_and_inverse(gram):
-    lower = jnp.linalg.cholesky(gram)
-    ident = jnp.eye(gram.shape[0], dtype=jnp.float32)
-    return (lower, jax.scipy.linalg.solve_triangular(lower, ident, lower=True))
+def factor_kernel(nb, gram, lower, inverse, work):
+    size = gram.shape[0]
+    tiles = size // 128
+    groups = nb // 8
+    lane = lax.broadcasted_iota(jnp.int32, (8, 128), 1)
+    sub = lax.broadcasted_iota(jnp.int32, (8, 128), 0)
+    for t in range(tiles):
+        work[t] = gram[:, 128 * t : 128 * (t + 1)]
+    for t in range(tiles):
+        r = lax.broadcasted_iota(jnp.int32, (size, 128), 0)
+        c = lax.broadcasted_iota(jnp.int32, (size, 128), 1) + 128 * t
+        work[tiles + t] = jnp.where(r == c, 1.0, 0.0)
+
+    def row(v, j):
+        return jnp.broadcast_to(v[j % 8 : j % 8 + 1], (8, 128))
+
+    for start in range(0, size, nb):
+        stop = start + nb
+        active = [t for t in range(tiles) if 128 * (t + 1) > start]
+        active += [tiles + t for t in range(tiles) if 128 * t < stop]
+        home = start // 128
+        panel = {
+            t: [work[t, start + 8 * g : start + 8 * g + 8] for g in range(groups)] for t in active
+        }
+        cols = [
+            [
+                jnp.broadcast_to(
+                    panel[home][g][:, start % 128 + k : start % 128 + k + 1], (8, 128)
+                )
+                for g in range(groups)
+            ]
+            for k in range(nb)
+        ]
+        recip = [jnp.ones((8, 128), jnp.float32)] * groups
+        pivots = [jnp.ones((8, 128), jnp.float32)] * groups
+        for j in range(nb):
+            home_group = j // 8
+            pivot = row(cols[j][home_group], j)
+            inv = 1.0 / pivot
+            at = sub == j % 8
+            recip[home_group] = jnp.where(at, inv, recip[home_group])
+            pivots[home_group] = jnp.where(at, pivot, pivots[home_group])
+            mult = [None] * groups
+            for g in range(home_group, groups):
+                mult[g] = cols[j][g] * inv
+                if g == home_group:
+                    mult[g] = jnp.where(sub > j % 8, mult[g], 0.0)
+            for k in range(j + 1, nb):
+                top = row(cols[k][home_group], j)
+                for g in range(home_group, groups):
+                    cols[k][g] = cols[k][g] - mult[g] * top
+            for t in active:
+                top = row(panel[t][home_group], j)
+                for g in range(home_group, groups):
+                    panel[t][g] = panel[t][g] - mult[g] * top
+        if stop < size:
+            full = {t: jnp.concatenate(panel[t], 0) if groups > 1 else panel[t][0] for t in active}
+            recips = jnp.concatenate(recip, 0) if groups > 1 else recip[0]
+            for u in range(tiles):
+                low = max(128 * u, stop)
+                if low >= 128 * (u + 1):
+                    continue
+                left = (full[u] * recips)[:, low - 128 * u :]
+                for t in active:
+                    if t < u:
+                        continue
+                    work[t, low : 128 * (u + 1)] -= lax.dot_general(
+                        left, full[t], (((0,), (0,)), ((), ())),
+                        precision=HIGHEST, preferred_element_type=jnp.float32)
+        for g in range(groups):
+            scale = 1.0 / jnp.sqrt(pivots[g])
+            at = slice(start + 8 * g, start + 8 * g + 8)
+            for t in range(tiles):
+                if t in active:
+                    keep = lane + 128 * t >= sub + (start + 8 * g)
+                    work[t, at] = jnp.where(keep, panel[t][g] * scale, 0.0)
+                else:
+                    work[t, at] = jnp.zeros((8, 128), jnp.float32)
+                if tiles + t in active:
+                    inverse[at, 128 * t : 128 * t + 128] = panel[tiles + t][g] * scale
+                else:
+                    inverse[at, 128 * t : 128 * t + 128] = jnp.zeros((8, 128), jnp.float32)
+    for t in range(tiles):
+        lower[128 * t : 128 * t + 128, :] = work[t].T
+
+def lower_and_inverse(gram, nb=16):
+    size = gram.shape[0]
+    vmem = pl.BlockSpec(memory_space=pltpu.VMEM)
+    return pl.pallas_call(
+        functools.partial(factor_kernel, nb),
+        out_shape=[jax.ShapeDtypeStruct((size, size), jnp.float32)] * 2,
+        in_specs=[vmem], out_specs=[vmem] * 2,
+        scratch_shapes=[pltpu.VMEM((2 * (size // 128), size, 128), jnp.float32)],
+        compiler_params=pltpu.CompilerParams(vmem_limit_bytes=32 << 20),
+    )(gram)
 
 
 def body(dims, block, onsite, hopping, cut_frac):

time: 250 us -> 146 us (0.58)
  other arithmetic: 109 us -> 0 us
  Pallas kernels: 122 us -> 141 us
  local copies, waits for them, and re-layouts: 11.9 us -> 3.42 us
  between operations: 4.21 us -> 1.34 us
  matrix products: 2.7 us -> 0 us
    another operation x20 -> x0, other arithmetic: 109 us -> none  [the longest x13 68.6 us: lower_and_inverse(): lower = jnp.linalg.cholesky(gram)]
    pallas_call x0 -> x2, Pallas kernels: none -> 20.5 us  [lower_and_inverse(): pl.pallas_call(functools.partial(factor_kernel, nb), out_shape=[jax.Shape...]
    another operation x19 -> x0, local copies, waits for them, and re-layouts: 8.22 us -> none  [the longest x15 8.17 us: lower_and_inverse(): return (lower, jax.scipy.linalg.solve_triangular(lower, ident, lower=True))]
    another operation x10 -> x0, matrix products: 2.7 us -> none  [the longest x6 1.75 us: lower_and_inverse(): return (lower, jax.scipy.linalg.solve_triangular(lower, ident, lower=True))]
where the time goes in v3:
time: 146 us
  Pallas kernels  141 us (97%)
  local copies, waits for them, and re-layouts  3.42 us (2%)
    pallas_call x3, Pallas kernels, call(): pl.pallas_call(kernel, out_shape=[jax.ShapeDtypeStruct(shape, jnp.float32...  121 us
    pallas_call x2, Pallas kernels, lower_and_inverse(): pl.pallas_call(functools.partial(factor_kernel, nb), out_shape=[jax.Shape...  20.5 us

profile of v3, /device:TPU:1, one launch (start us, length us, event | category | flops | bytes accessed | tf_op | source)
XLA Modules:
  0.0 146.2 jit_solution(3484835902771366107)
XLA Ops:
  1.3 0.0 copy-start.1
  1.3 0.9 broadcast_in_dim.2.onsite
  2.2 0.0 copy-done.1
  2.2 0.0 copy-start
  2.2 1.0 copy-done
  3.2 68.8 %shard_map.67 = (f32[512,256]{1,0:T(8,128)S(1)}, f32[256,256]{1,0:T(8,128)S(1)}) custom-call(f32[8,8,8,256]{3,2,1,0:T(8,128)S(1)} %copy-done, f32[8,8,8,128]{3,2,1,0:T(8,128)S(1)} %broadcast_in_dim.2.onsite, f32[13]{0:T(128)S(1)} %copy-done.1, f32[1]{0:T(128)S(6)} %copy.9.cut_frac), custom_call_target="tpu_custom_call" | custom-call | tf_op jit(solution)/shard_map/pallas_call | solution.py:506
  72.1 10.2 %shard_map.68 = (f32[256,256]{1,0:T(8,128)}, f32[256,256]{1,0:T(8,128)S(1)}) custom-call(f32[256,256]{1,0:T(8,128)S(1)} %get-tuple-element.13.gram), custom_call_target="tpu_custom_call" | custom-call | tf_op jit(solution)/shard_map/pallas_call | solution.py:606
  82.3 20.1 %shard_map.69 = (f32[512,256]{1,0:T(8,128)S(1)}, f32[256,256]{1,0:T(8,128)S(1)}) custom-call(f32[512,256]{1,0:T(8,128)S(1)} %get-tuple-element.12.flat, f32[256,256]{1,0:T(8,128)S(1)} %get-tuple-element.14.factor), custom_call_target="tpu_custom_call" | custom-call | tf_op jit(solution)/shard_map/pallas_call | solution.py:506
  102.4 10.2 %shard_map.70 = (f32[256,256]{1,0:T(8,128)}, f32[256,256]{1,0:T(8,128)S(1)}) custom-call(f32[256,256]{1,0:T(8,128)S(1)} %get-tuple-element.16.gram), custom_call_target="tpu_custom_call" | custom-call | tf_op jit(solution)/shard_map/pallas_call | solution.py:606
  112.6 32.0 %shard_map.71 = (f32[512,256]{1,0:T(8,128)S(1)}, f32[256,256]{1,0:T(8,128)S(1)}) custom-call(f32[512,256]{1,0:T(8,128)S(1)} %get-tuple-element.15.first, f32[256,256]{1,0:T(8,128)S(1)} %get-tuple-element.17.factor, f32[8,8,8,128]{3,2,1,0:T(8,128)S(1)} %broadcast_in_dim.2.onsite, f32[13]{0:T(128)S(1)} %copy-done.1), custom_call_target="tpu_custom_call" | custom-call | tf_op jit(solution)/shard_map/pallas_call | solution.py:506
  144.7 0.8 copy.10
  145.5 0.7 copy.11
Async XLA Ops:
  1.3 0.9 copy-start.1
  2.2 1.0 copy-start

commit v4 on v3

--- a/solution.py
+++ b/solution.py
@@ -8,6 +8,7 @@
 from jax.sharding import PartitionSpec as P
 
 DEG = 4
+PANEL = 16
 MESH = pl.DeviceIdType.MESH
 HIGHEST = lax.Precision.HIGHEST
 AXES = ("gx", "gy", "gz")
@@ -98,44 +99,60 @@
     ).start()
 
 
-def all_reduce(dims, local, total, plane_buf, column_buf, sems):
-    plane, column = dims[0] * dims[2], dims[1]
-    rows = local.shape[0] // plane
-    place = lax.axis_index("gx") * dims[2] + lax.axis_index("gz")
-    level = lax.axis_index("gy")
-    mine = pl.ds(pl.multiple_of(place * rows, rows), rows)
-
-    @pl.loop(1, plane)
-    def _(k):
-        peer, device = plane_peer(dims, k)
-        theirs = pl.ds(pl.multiple_of(peer * rows, rows), rows)
-        send(local.at[theirs], plane_buf.at[k - 1], sems.at[0], sems.at[1], device)
-
-    wait_bytes(plane_buf, sems.at[1])
-    column_buf[level] = lax.fori_loop(
-        0, plane - 1, lambda k, acc: acc + plane_buf[k], local[mine]
-    )
-
-    @pl.loop(1, column)
-    def _(k):
-        _, device = column_peer(dims, k)
-        send(column_buf.at[level], column_buf.at[level], sems.at[2], sems.at[3], device)
-
-    wait_bytes(column_buf.at[pl.ds(0, column - 1)], sems.at[3])
-    part = column_buf[0]
-    for k in range(1, column):
-        part = part + column_buf[k]
-    total[mine] = part
-
-    @pl.loop(1, plane)
-    def _(k):
-        _, device = plane_peer(dims, k)
-        send(total.at[mine], total.at[mine], sems.at[4], sems.at[5], device)
-
-    wait_bytes(total.at[pl.ds(0, (plane - 1) * rows)], sems.at[5])
-    wait_bytes(plane_buf, sems.at[0])
-    wait_bytes(column_buf.at[pl.ds(0, column - 1)], sems.at[2])
-    wait_bytes(total.at[pl.ds(0, (plane - 1) * rows)], sems.at[4])
+def place_of(dims):
+    return lax.axis_index("gx") * dims[2] + lax.axis_index("gz")
+
+
+class AllReduce:
+    def __init__(self, dims, local, total, plane_buf, column_buf, sems):
+        self.dims, self.local, self.total = dims, local, total
+        self.plane_buf, self.column_buf, self.sems = plane_buf, column_buf, sems
+        self.plane, self.column = dims[0] * dims[2], dims[1]
+        self.rows = local.shape[0] // self.plane
+        self.mine = pl.ds(pl.multiple_of(place_of(dims) * self.rows, self.rows), self.rows)
+
+    def scatter(self):
+        @pl.loop(1, self.plane)
+        def _(k):
+            peer, device = plane_peer(self.dims, k)
+            theirs = pl.ds(pl.multiple_of(peer * self.rows, self.rows), self.rows)
+            send(
+                self.local.at[theirs], self.plane_buf.at[k - 1],
+                self.sems.at[0], self.sems.at[1], device,
+            )
+
+    def across(self):
+        level = lax.axis_index("gy")
+        wait_bytes(self.plane_buf, self.sems.at[1])
+        self.column_buf[level] = lax.fori_loop(
+            0, self.plane - 1, lambda k, acc: acc + self.plane_buf[k], self.local[self.mine]
+        )
+        mine = self.column_buf.at[level]
+
+        @pl.loop(1, self.column)
+        def _(k):
+            _, device = column_peer(self.dims, k)
+            send(mine, mine, self.sems.at[2], self.sems.at[3], device)
+
+    def gather(self):
+        wait_bytes(self.column_buf.at[pl.ds(0, self.column - 1)], self.sems.at[3])
+        part = self.column_buf[0]
+        for k in range(1, self.column):
+            part = part + self.column_buf[k]
+        self.total[self.mine] = part
+        mine = self.total.at[self.mine]
+
+        @pl.loop(1, self.plane)
+        def _(k):
+            _, device = plane_peer(self.dims, k)
+            send(mine, mine, self.sems.at[4], self.sems.at[5], device)
+
+    def finish(self):
+        others = self.total.at[pl.ds(0, (self.plane - 1) * self.rows)]
+        wait_bytes(others, self.sems.at[5])
+        wait_bytes(self.plane_buf, self.sems.at[0])
+        wait_bytes(self.column_buf.at[pl.ds(0, self.column - 1)], self.sems.at[2])
+        wait_bytes(others, self.sems.at[4])
 
 
 def reduce_scratch(dims, size):
@@ -353,7 +370,7 @@
 def filter_kernel(
     dims, shape, sites,
     block, onsite, hopping, cut_frac,
-    flat, gram,
+    flat, image, gram,
     field, face, edge, corner, face_out, edge_out, corner_out, shifted, halo_sems,
     max_plane, max_column, max_sems, coef,
     local, total, plane_buf, column_buf, sums_sems,
@@ -415,17 +432,36 @@
                     older = field[after, x + 1, y + 1]
                     value = wide(2 * step) * value - wide(2 * step + 1) * older
                 if step == DEG - 1:
-                    flat[pl.ds(pl.multiple_of((x * size_y + y) * size_z, size_z), size_z)] = value
-                else:
-                    field[after, x + 1, y + 1] = value
-                    pack_column(shape, after, x, y, value, face_out, edge_out)
-
-        if step < DEG - 1:
-            pack_corners(shape, after, field, corner_out)
-    halo_wait(dims, shape, (DEG - 1) % 2, refs, halo_sems, False)
+                    flat[site_rows(shape, x, y)] = value
+                field[after, x + 1, y + 1] = value
+                pack_column(shape, after, x, y, value, face_out, edge_out)
+
+        pack_corners(shape, after, field, corner_out)
+    slot = DEG % 2
+    sums = AllReduce(dims, local, total, plane_buf, column_buf, sums_sems)
+    halo_send(dims, shape, slot, refs, halo_sems)
     local[...] = product(flat[...], flat[...])
-    all_reduce(dims, local, total, plane_buf, column_buf, sums_sems)
+    sums.scatter()
+    halo_wait(dims, shape, slot, refs, halo_sems, True)
+    shift_columns(shape, slot, field, face, edge, corner, shifted)
+    sums.across()
+
+    @pl.loop(0, size_x)
+    def _(x):
+        totals, _ = apply_rows(shape, slot, x, field, shifted, onsite, hopping)
+        for y in range(size_y):
+            image[site_rows(shape, x, y)] = totals[y]
+
+    sums.gather()
+    halo_wait(dims, shape, 1 - slot, refs, halo_sems, False)
+    halo_wait(dims, shape, slot, refs, halo_sems, False)
+    sums.finish()
     gram[...] = total[...] / sites
+
+
+def site_rows(shape, x, y):
+    _, size_y, size_z, _ = shape
+    return pl.ds(pl.multiple_of((x * size_y + y) * size_z, size_z), size_z)
 
 
 def product(left, right):
@@ -449,55 +485,31 @@
 
 
 def rotate_kernel(
-    dims, sites, flat, factor, first, gram, local, total, plane_buf, column_buf, sums_sems
+    dims, sites,
+    flat, image, factor,
+    first, gram, between,
+    moved,
+    local, total, plane_buf, column_buf, sums_sems,
+    local_b, total_b, plane_buf_b, column_buf_b, sums_sems_b,
 ):
     enter(dims, False)
+    sums = AllReduce(dims, local, total, plane_buf, column_buf, sums_sems)
+    sums_b = AllReduce(dims, local_b, total_b, plane_buf_b, column_buf_b, sums_sems_b)
     first[...] = rotated(flat[...], factor[...])
     local[...] = product(first[...], first[...])
     entered(dims, False)
-    all_reduce(dims, local, total, plane_buf, column_buf, sums_sems)
+    sums.scatter()
+    moved[...] = rotated(image[...], factor[...])
+    local_b[...] = product(first[...], moved[...])
+    sums_b.scatter()
+    sums.across()
+    sums_b.across()
+    sums.gather()
+    sums_b.gather()
+    sums.finish()
     gram[...] = total[...] / sites
-
-
-def project_kernel(
-    dims, shape, sites,
-    first, factor, onsite, hopping,
-    states, gram,
-    field, face, edge, corner, face_out, edge_out, corner_out, shifted, halo_sems, image,
-    local, total, plane_buf, column_buf, sums_sems,
-):
-    size_x, size_y, size_z, columns = shape
-    refs = (field, face, edge, corner, face_out, edge_out, corner_out)
-    zero_border(dims, shape, 1, field, face, edge, corner)
-    enter(dims, True)
-    states[...] = rotated(first[...], factor[...])
-
-    def rows(x, y):
-        return pl.ds(pl.multiple_of((x * size_y + y) * size_z, size_z), size_z)
-
-    @pl.loop(0, size_x)
-    def _(x):
-        for y in range(size_y):
-            value = states[rows(x, y)]
-            field[0, x + 1, y + 1] = value
-            pack_column(shape, 0, x, y, value, face_out, edge_out)
-
-    pack_corners(shape, 0, field, corner_out)
-    entered(dims, True)
-    halo_send(dims, shape, 0, refs, halo_sems)
-    halo_wait(dims, shape, 0, refs, halo_sems, True)
-    shift_columns(shape, 0, field, face, edge, corner, shifted)
-
-    @pl.loop(0, size_x)
-    def _(x):
-        totals, _ = apply_rows(shape, 0, x, field, shifted, onsite, hopping)
-        for y in range(size_y):
-            image[rows(x, y)] = totals[y]
-
-    halo_wait(dims, shape, 0, refs, halo_sems, False)
-    local[...] = product(states[...], image[...])
-    all_reduce(dims, local, total, plane_buf, column_buf, sums_sems)
-    gram[...] = total[...] / sites
+    sums_b.finish()
+    between[...] = total_b[...] / sites
 
 
 def call(kernel, inputs, scalars, outputs, scratch, ident):
@@ -600,16 +612,25 @@
     for t in range(tiles):
         lower[128 * t : 128 * t + 128, :] = work[t].T
 
-def lower_and_inverse(gram, nb=16):
-    size = gram.shape[0]
+def finish_kernel(nb, gram, first, between, states, projected, lower, inverse, work):
+    factor_kernel(nb, gram, lower, inverse, work)
+    states[...] = rotated(first[...], inverse[...])
+    half = rotated(between[...], inverse[...])
+    projected[...] = jnp.dot(
+        inverse[...], half, precision=HIGHEST, preferred_element_type=jnp.float32
+    )
+
+
+def local_call(kernel, inputs, outputs, scratch):
     vmem = pl.BlockSpec(memory_space=pltpu.VMEM)
     return pl.pallas_call(
-        functools.partial(factor_kernel, nb),
-        out_shape=[jax.ShapeDtypeStruct((size, size), jnp.float32)] * 2,
-        in_specs=[vmem], out_specs=[vmem] * 2,
-        scratch_shapes=[pltpu.VMEM((2 * (size // 128), size, 128), jnp.float32)],
+        kernel,
+        out_shape=[jax.ShapeDtypeStruct(shape, jnp.float32) for shape in outputs],
+        in_specs=[vmem] * len(inputs),
+        out_specs=[vmem] * len(outputs),
+        scratch_shapes=scratch,
         compiler_params=pltpu.CompilerParams(vmem_limit_bytes=32 << 20),
-    )(gram)
+    )(*inputs)
 
 
 def body(dims, block, onsite, hopping, cut_frac):
@@ -620,11 +641,13 @@
     plane, column = dims[0] * dims[2], dims[1]
     sums = reduce_scratch(dims, columns)
     levels = jnp.broadcast_to(onsite[..., None], onsite.shape + (128,))
-    flat, gram_one = call(
+    square = (columns, columns)
+    work = pltpu.VMEM((2 * (columns // 128), columns, 128), jnp.float32)
+    flat, image, gram_one = call(
         functools.partial(filter_kernel, dims, shape, sites),
         [block, levels],
         [hopping, cut_frac],
-        [(count, columns), (columns, columns)],
+        [(count, columns), (count, columns), square],
         halo_scratch(shape, 2)
         + [
             pltpu.VMEM((plane, 8, 128), jnp.float32),
@@ -635,23 +658,22 @@
         + sums,
         1,
     )
-    lower_one, inverse_one = lower_and_inverse(gram_one)
-    first, gram_two = call(
+    lower_one, inverse_one = local_call(
+        functools.partial(factor_kernel, PANEL), [gram_one], [square, square], [work]
+    )
+    first, gram_two, between = call(
         functools.partial(rotate_kernel, dims, sites),
-        [flat, inverse_one],
+        [flat, image, inverse_one],
         [],
-        [(count, columns), (columns, columns)],
-        sums,
+        [(count, columns), square, square],
+        [pltpu.VMEM((count, columns), jnp.float32)] + sums + sums,
         2,
     )
-    _, inverse_two = lower_and_inverse(gram_two)
-    states, projected = call(
-        functools.partial(project_kernel, dims, shape, sites),
-        [first, inverse_two, levels],
-        [hopping],
-        [(count, columns), (columns, columns)],
-        halo_scratch(shape, 1) + [pltpu.VMEM((count, columns), jnp.float32)] + sums,
-        3,
+    states, projected = local_call(
+        functools.partial(finish_kernel, PANEL),
+        [gram_two, first, between],
+        [(count, columns), square],
+        [pltpu.VMEM(square, jnp.float32), pltpu.VMEM(square, jnp.float32), work],
     )
     return (states.reshape(shape), projected, lower_one)
 

time: 146 us -> 120 us (0.82)
  Pallas kernels: 141 us -> 116 us
  local copies, waits for them, and re-layouts: 3.42 us -> 1.93 us
    pallas_call x3 -> x2, Pallas kernels: 121 us -> 94.8 us  [call(): pl.pallas_call(kernel, out_shape=[jax.ShapeDtypeStruct(shape, jnp.float32...]
    unnamed x6 -> x4, local copies, waits for them, and re-layouts: 2.54 us -> 1.04 us
where the time goes in v4:
time: 120 us
  Pallas kernels  116 us (97%)
  local copies, waits for them, and re-layouts  1.93 us (2%)
  between operations  1.33 us (1%)
    pallas_call x2, Pallas kernels, call(): pl.pallas_call(kernel, out_shape=[jax.ShapeDtypeStruct(shape, jnp.float32...  94.8 us
    pallas_call x2, Pallas kernels, local_call(): pl.pallas_call(kernel, out_shape=[jax.ShapeDtypeStruct(shape, jnp.float32...  21.6 us

profile of v4, /device:TPU:1, one launch (start us, length us, event | category | flops | bytes accessed | tf_op | source)
XLA Modules:
  0.0 119.6 jit_solution(11048120655971943622)
XLA Ops:
  1.3 0.0 copy-start.1
  1.3 0.9 broadcast_in_dim.2.onsite
  2.2 0.0 copy-done.1
  2.2 0.0 copy-start
  2.2 1.0 copy-done
  3.2 70.6 %shard_map.67 = (f32[512,256]{1,0:T(8,128)S(1)}, f32[512,256]{1,0:T(8,128)S(1)}, f32[256,256]{1,0:T(8,128)S(1)}) custom-call(f32[8,8,8,256]{3,2,1,0:T(8,128)S(1)} %copy-done, f32[8,8,8,128]{3,2,1,0:T(8,128)S(1)} %broadcast_in_dim.2.onsite, f32[13]{0:T(128)S(1)} %copy-done.1, f32[1]{0:T(128)S(6)} %copy.7.cut_frac), custom_call_target="tpu_custom_call" | custom-call | tf_op jit(solution)/shard_map/pallas_call | solution.py:518
  73.9 10.2 %shard_map.68 = (f32[256,256]{1,0:T(8,128)}, f32[256,256]{1,0:T(8,128)S(1)}) custom-call(f32[256,256]{1,0:T(8,128)S(1)} %get-tuple-element.15.gram), custom_call_target="tpu_custom_call" | custom-call | tf_op jit(solution)/shard_map/pallas_call | solution.py:626
  84.1 24.2 %shard_map.69 = (f32[512,256]{1,0:T(8,128)S(1)}, f32[256,256]{1,0:T(8,128)S(1)}, f32[256,256]{1,0:T(8,128)S(1)}) custom-call(f32[512,256]{1,0:T(8,128)S(1)} %get-tuple-element.13.flat, f32[512,256]{1,0:T(8,128)S(1)} %get-tuple-element.14.image, f32[256,256]{1,0:T(8,128)S(1)} %get-tuple-element.16.factor), custom_call_target="tpu_custom_call" | custom-call | tf_op jit(solution)/shard_map/pallas_call | solution.py:518
  108.3 11.3 %shard_map.70 = (f32[512,256]{1,0:T(8,128)}, f32[256,256]{1,0:T(8,128)}) custom-call(f32[256,256]{1,0:T(8,128)S(1)} %get-tuple-element.17.gram, f32[512,256]{1,0:T(8,128)S(1)} %get-tuple-element.18.first, f32[256,256]{1,0:T(8,128)S(1)} %get-tuple-element.19.between), custom_call_target="tpu_custom_call" | custom-call | tf_op jit(solution)/shard_map/pallas_call | solution.py:626
Async XLA Ops:
  1.3 0.9 copy-start.1
  2.2 1.0 copy-start

commit v5 on v4

--- a/solution.py
+++ b/solution.py
@@ -9,6 +9,8 @@
 
 DEG = 4
 PANEL = 16
+HALVES = 2
+HALO_REFS = 9
 MESH = pl.DeviceIdType.MESH
 HIGHEST = lax.Precision.HIGHEST
 AXES = ("gx", "gy", "gz")
@@ -343,7 +345,7 @@
 
 
 def apply_rows(shape, slot, x, field, shifted, onsite, hopping):
-    size_y, columns = shape[1], shape[3]
+    size_y = shape[1]
     totals = [None] * size_y
     centres = [None] * size_y
     for dx in (-1, 0, 1):
@@ -360,101 +362,136 @@
                     if (dx, dy, dz) == (0, 0, 0):
                         centres[target] = value
                         level = onsite[x, target]
-                        term = jnp.concatenate([level] * (columns // level.shape[1]), 1) * value
+                        term = level * value
                     else:
                         term = hopping[hop_index((dx, dy, dz))] * value
                     totals[target] = term if totals[target] is None else totals[target] + term
     return totals, centres
 
 
-def filter_kernel(
-    dims, shape, sites,
-    block, onsite, hopping, cut_frac,
-    flat, image, gram,
-    field, face, edge, corner, face_out, edge_out, corner_out, shifted, halo_sems,
-    max_plane, max_column, max_sems, coef,
-    local, total, plane_buf, column_buf, sums_sems,
-):
-    size_x, size_y, size_z, columns = shape
-    refs = (field, face, edge, corner, face_out, edge_out, corner_out)
-    zero_border(dims, shape, 2, field, face, edge, corner)
-    enter(dims, True)
-    place = lax.axis_index("gx") * dims[2] + lax.axis_index("gz")
-    max_plane[place] = jnp.full((8, 128), jnp.max(jnp.abs(onsite[...])), jnp.float32)
+def spread(onsite, levels):
+    size_x, size_y, size_z, lanes = levels.shape
+    diagonal = lax.broadcasted_iota(jnp.int32, (size_z, size_z), 0) == lax.broadcasted_iota(
+        jnp.int32, (size_z, size_z), 1
+    )
 
     @pl.loop(0, size_x)
     def _(x):
         for y in range(size_y):
-            value = block[x, y]
-            field[0, x + 1, y + 1] = value
-            pack_column(shape, 0, x, y, value, face_out, edge_out)
-
-    pack_corners(shape, 0, field, corner_out)
+            row = jnp.broadcast_to(onsite[x, y : y + 1], (size_z, size_z))
+            column = jnp.sum(jnp.where(diagonal, row, 0.0), axis=1, keepdims=True)
+            levels[x, y] = jnp.broadcast_to(column, (size_z, lanes))
+
+
+def filter_coefficients(bound, cut_frac, coef):
+    cut = cut_frac * bound
+    half_width = (bound - cut) / 2.0
+    center = (bound + cut) / 2.0
+    sigma_one = half_width / (-bound - center)
+    sigma = sigma_one
+    coef[0] = center
+    coef[1] = sigma / half_width
+    for k in range(1, DEG):
+        sigma_next = 1.0 / (2.0 / sigma_one - sigma)
+        coef[2 * k] = 2.0 * sigma_next / half_width
+        coef[2 * k + 1] = sigma * sigma_next
+        sigma = sigma_next
+
+
+def filter_kernel(dims, shape, sites, block, onsite, hopping, cut_frac, flat, image, gram, *scratch):
+    size_x, size_y, size_z, lanes = shape
+    per_half = HALO_REFS
+    halves = []
+    for half in range(HALVES):
+        *refs, shifted, sems = scratch[half * per_half : (half + 1) * per_half]
+        halves.append((tuple(refs), shifted, sems))
+    (
+        onsite_here, levels, input_sems,
+        max_plane, max_column, max_sems, coef,
+        local, total, plane_buf, column_buf, sums_sems,
+    ) = scratch[HALVES * per_half :]
+    enter(dims, True)
+    copies = [pltpu.make_async_copy(onsite, onsite_here, input_sems.at[HALVES])]
+    for half, (refs, _, _) in enumerate(halves):
+        inside = refs[0].at[0, pl.ds(1, size_x), pl.ds(1, size_y)]
+        source = block.at[:, :, :, pl.ds(lanes * half, lanes)]
+        copies.append(pltpu.make_async_copy(source, inside, input_sems.at[half]))
+    for copy in copies:
+        copy.start()
+    for refs, _, _ in halves:
+        zero_border(dims, shape, 2, *refs[:4])
+    copies[0].wait()
+    place = place_of(dims)
+    max_plane[place] = jnp.full((8, 128), jnp.max(jnp.abs(onsite_here[...])), jnp.float32)
+    for copy, (refs, _, _) in zip(copies[1:], halves):
+        copy.wait()
+        field, face_out, edge_out, corner_out = refs[0], *refs[4:]
+
+        @pl.loop(0, size_x)
+        def _(x):
+            for y in range(size_y):
+                pack_column(shape, 0, x, y, field[0, x + 1, y + 1], face_out, edge_out)
+
+        pack_corners(shape, 0, field, corner_out)
+    spread(onsite_here, levels)
     entered(dims, True)
+    for index, (refs, _, sems) in enumerate(halves):
+        halo_send(dims, shape, 0, refs, sems)
+        if index == 0:
+            max_start(dims, None, max_plane, max_sems)
+    max_middle(dims, max_plane, max_column, max_sems)
     for step in range(DEG):
         slot, after = step % 2, (step + 1) % 2
-        halo_send(dims, shape, slot, refs, halo_sems)
-        if step == 0:
-            max_start(dims, None, max_plane, max_sems)
-            max_middle(dims, max_plane, max_column, max_sems)
-        halo_wait(dims, shape, slot, refs, halo_sems, True)
-        shift_columns(shape, slot, field, face, edge, corner, shifted)
-        if step == 0:
-            bound = max_end(dims, max_plane, max_column, max_sems)
-            reach = jnp.abs(hopping[0])
-            for k in range(1, len(POSITIVE)):
-                reach = reach + jnp.abs(hopping[k])
-            bound = bound + 2.0 * reach
-            cut = cut_frac[0] * bound
-            half_width = (bound - cut) / 2.0
-            center = (bound + cut) / 2.0
-            sigma_one = half_width / (-bound - center)
-            sigma = sigma_one
-            coef[0] = center
-            coef[1] = sigma / half_width
-            for k in range(1, DEG):
-                sigma_next = 1.0 / (2.0 / sigma_one - sigma)
-                coef[2 * k] = 2.0 * sigma_next / half_width
-                coef[2 * k + 1] = sigma * sigma_next
-                sigma = sigma_next
-        if step:
-            halo_wait(dims, shape, after, refs, halo_sems, False)
+        for half, (refs, shifted, sems) in enumerate(halves):
+            field, face, edge, corner, face_out, edge_out, corner_out = refs
+            halo_wait(dims, shape, slot, refs, sems, True)
+            shift_columns(shape, slot, field, face, edge, corner, shifted)
+            if step == 0 and half == 0:
+                reach = jnp.abs(hopping[0])
+                for k in range(1, len(POSITIVE)):
+                    reach = reach + jnp.abs(hopping[k])
+                bound = max_end(dims, max_plane, max_column, max_sems) + 2.0 * reach
+                filter_coefficients(bound, cut_frac[0], coef)
+            if step:
+                halo_wait(dims, shape, after, refs, sems, False)
+
+            @pl.loop(0, size_x)
+            def _(x):
+                totals, centres = apply_rows(shape, slot, x, field, shifted, levels, hopping)
+                for y in range(size_y):
+                    value = totals[y] - coef[0] * centres[y]
+                    if step == 0:
+                        value = coef[1] * value
+                    else:
+                        older = field[after, x + 1, y + 1]
+                        value = coef[2 * step] * value - coef[2 * step + 1] * older
+                    if step == DEG - 1:
+                        flat[site_rows(shape, x, y), lanes * half : lanes * (half + 1)] = value
+                    field[after, x + 1, y + 1] = value
+                    pack_column(shape, after, x, y, value, face_out, edge_out)
+
+            pack_corners(shape, after, field, corner_out)
+            halo_send(dims, shape, after, refs, sems)
+    slot = DEG % 2
+    sums = AllReduce(dims, local, total, plane_buf, column_buf, sums_sems)
+    local[...] = product(flat[...], flat[...])
+    sums.scatter()
+    for refs, shifted, sems in halves:
+        halo_wait(dims, shape, slot, refs, sems, True)
+        shift_columns(shape, slot, *refs[:4], shifted)
+    sums.across()
+    for half, (refs, shifted, sems) in enumerate(halves):
 
         @pl.loop(0, size_x)
         def _(x):
-            wide = lambda k: jnp.concatenate([coef[k]] * (columns // 128), 1)
-            totals, centres = apply_rows(shape, slot, x, field, shifted, onsite, hopping)
+            totals, _ = apply_rows(shape, slot, x, refs[0], shifted, levels, hopping)
             for y in range(size_y):
-                value = totals[y] - wide(0) * centres[y]
-                if step == 0:
-                    value = wide(1) * value
-                else:
-                    older = field[after, x + 1, y + 1]
-                    value = wide(2 * step) * value - wide(2 * step + 1) * older
-                if step == DEG - 1:
-                    flat[site_rows(shape, x, y)] = value
-                field[after, x + 1, y + 1] = value
-                pack_column(shape, after, x, y, value, face_out, edge_out)
-
-        pack_corners(shape, after, field, corner_out)
-    slot = DEG % 2
-    sums = AllReduce(dims, local, total, plane_buf, column_buf, sums_sems)
-    halo_send(dims, shape, slot, refs, halo_sems)
-    local[...] = product(flat[...], flat[...])
-    sums.scatter()
-    halo_wait(dims, shape, slot, refs, halo_sems, True)
-    shift_columns(shape, slot, field, face, edge, corner, shifted)
-    sums.across()
-
-    @pl.loop(0, size_x)
-    def _(x):
-        totals, _ = apply_rows(shape, slot, x, field, shifted, onsite, hopping)
-        for y in range(size_y):
-            image[site_rows(shape, x, y)] = totals[y]
+                image[site_rows(shape, x, y), lanes * half : lanes * (half + 1)] = totals[y]
 
     sums.gather()
-    halo_wait(dims, shape, 1 - slot, refs, halo_sems, False)
-    halo_wait(dims, shape, slot, refs, halo_sems, False)
+    for refs, _, sems in halves:
+        halo_wait(dims, shape, 1 - slot, refs, sems, False)
+        halo_wait(dims, shape, slot, refs, sems, False)
     sums.finish()
     gram[...] = total[...] / sites
 
@@ -512,13 +549,13 @@
     between[...] = total_b[...] / sites
 
 
-def call(kernel, inputs, scalars, outputs, scratch, ident):
+def call(kernel, inputs, scalars, outputs, scratch, ident, space=pltpu.VMEM):
     vmem = pl.BlockSpec(memory_space=pltpu.VMEM)
     smem = pl.BlockSpec(memory_space=pltpu.SMEM)
     return pl.pallas_call(
         kernel,
         out_shape=[jax.ShapeDtypeStruct(shape, jnp.float32) for shape in outputs],
-        in_specs=[vmem] * len(inputs) + [smem] * len(scalars),
+        in_specs=[pl.BlockSpec(memory_space=space)] * len(inputs) + [smem] * len(scalars),
         out_specs=[vmem] * len(outputs),
         scratch_shapes=scratch,
         compiler_params=pltpu.CompilerParams(
@@ -640,16 +677,20 @@
     sites = count * dims[0] * dims[1] * dims[2]
     plane, column = dims[0] * dims[2], dims[1]
     sums = reduce_scratch(dims, columns)
-    levels = jnp.broadcast_to(onsite[..., None], onsite.shape + (128,))
     square = (columns, columns)
     work = pltpu.VMEM((2 * (columns // 128), columns, 128), jnp.float32)
+    lanes = columns // HALVES
+    part = (size_x, size_y, size_z, lanes)
     flat, image, gram_one = call(
-        functools.partial(filter_kernel, dims, shape, sites),
-        [block, levels],
+        functools.partial(filter_kernel, dims, part, sites),
+        [block, onsite],
         [hopping, cut_frac],
         [(count, columns), (count, columns), square],
-        halo_scratch(shape, 2)
+        halo_scratch(part, 2) * HALVES
         + [
+            pltpu.VMEM((size_x, size_y, size_z), jnp.float32),
+            pltpu.VMEM(part, jnp.float32),
+            pltpu.SemaphoreType.DMA((HALVES + 1,)),
             pltpu.VMEM((plane, 8, 128), jnp.float32),
             pltpu.VMEM((column, 8, 128), jnp.float32),
             pltpu.SemaphoreType.DMA((4,)),
@@ -657,6 +698,7 @@
         ]
         + sums,
         1,
+        pltpu.HBM,
     )
     lower_one, inverse_one = local_call(
         functools.partial(factor_kernel, PANEL), [gram_one], [square, square], [work]

time: 120 us -> 116 us (0.967)
  Pallas kernels: 116 us -> 113 us
    pallas_call x2, Pallas kernels: 94.8 us -> 91 us  [call(): pl.pallas_call(kernel, out_shape=[jax.ShapeDtypeStruct(shape, jnp.float32...]
where the time goes in v5:
time: 116 us
  Pallas kernels  113 us (97%)
  local copies, waits for them, and re-layouts  1.8 us (2%)
  between operations  1.33 us (1%)
    pallas_call x2, Pallas kernels, call(): pl.pallas_call(kernel, out_shape=[jax.ShapeDtypeStruct(shape, jnp.float32...  91 us
    pallas_call x2, Pallas kernels, local_call(): pl.pallas_call(kernel, out_shape=[jax.ShapeDtypeStruct(shape, jnp.float32...  21.6 us

profile of v5, /device:TPU:1, one launch (start us, length us, event | category | flops | bytes accessed | tf_op | source)
XLA Modules:
  0.0 115.7 jit_solution(4914662301035186561)
XLA Ops:
  0.6 0.0 copy-start.2
  1.3 0.0 copy-done.2
  1.3 0.0 copy-start
  1.3 1.0 copy-done
  2.4 0.0 copy-start.1
  2.4 0.8 copy-done.1
  3.1 67.0 %shard_map.67 = (f32[512,256]{1,0:T(8,128)S(1)}, f32[512,256]{1,0:T(8,128)S(1)}, f32[256,256]{1,0:T(8,128)S(1)}) custom-call(f32[8,8,8,256]{3,2,1,0:T(8,128)S(1)} %copy-done, f32[8,8,8]{2,1,0:T(8,128)S(1)} %copy-done.1, f32[13]{0:T(128)S(1)} %copy-done.2, f32[1]{0:T(128)S(6)} %copy.7.cut_frac), custom_call_target="tpu_custom_call" | custom-call | tf_op jit(solution)/shard_map/pallas_call | solution.py:555
  70.1 10.2 %shard_map.68 = (f32[256,256]{1,0:T(8,128)}, f32[256,256]{1,0:T(8,128)S(1)}) custom-call(f32[256,256]{1,0:T(8,128)S(1)} %get-tuple-element.15.gram), custom_call_target="tpu_custom_call" | custom-call | tf_op jit(solution)/shard_map/pallas_call | solution.py:663
  80.4 24.0 %shard_map.69 = (f32[512,256]{1,0:T(8,128)S(1)}, f32[256,256]{1,0:T(8,128)S(1)}, f32[256,256]{1,0:T(8,128)S(1)}) custom-call(f32[512,256]{1,0:T(8,128)S(1)} %get-tuple-element.13.flat, f32[512,256]{1,0:T(8,128)S(1)} %get-tuple-element.14.image, f32[256,256]{1,0:T(8,128)S(1)} %get-tuple-element.16.factor), custom_call_target="tpu_custom_call" | custom-call | tf_op jit(solution)/shard_map/pallas_call | solution.py:555
  104.4 11.3 %shard_map.70 = (f32[512,256]{1,0:T(8,128)}, f32[256,256]{1,0:T(8,128)}) custom-call(f32[256,256]{1,0:T(8,128)S(1)} %get-tuple-element.17.gram, f32[512,256]{1,0:T(8,128)S(1)} %get-tuple-element.18.first, f32[256,256]{1,0:T(8,128)S(1)} %get-tuple-element.19.between), custom_call_target="tpu_custom_call" | custom-call | tf_op jit(solution)/shard_map/pallas_call | solution.py:663
Async XLA Ops:
  0.6 0.7 copy-start.2
  1.3 1.0 copy-start
  2.4 0.8 copy-start.1

commit v6 on v5

--- a/solution.py
+++ b/solution.py
@@ -9,6 +9,8 @@
 
 DEG = 4
 PANEL = 16
+NEAR_STEPS = 4
+NEAR_LEFT = 1e-3
 HALVES = 2
 HALO_REFS = 9
 MESH = pl.DeviceIdType.MESH
@@ -523,15 +525,16 @@
 
 def rotate_kernel(
     dims, sites,
-    flat, image, factor,
-    first, gram, between,
-    moved,
+    flat, image, gram_one,
+    first, gram, between, lower,
+    factor, work, moved,
     local, total, plane_buf, column_buf, sums_sems,
     local_b, total_b, plane_buf_b, column_buf_b, sums_sems_b,
 ):
     enter(dims, False)
     sums = AllReduce(dims, local, total, plane_buf, column_buf, sums_sems)
     sums_b = AllReduce(dims, local_b, total_b, plane_buf_b, column_buf_b, sums_sems_b)
+    factor_kernel(PANEL, gram_one, lower, factor, work)
     first[...] = rotated(flat[...], factor[...])
     local[...] = product(first[...], first[...])
     entered(dims, False)
@@ -649,8 +652,41 @@
     for t in range(tiles):
         lower[128 * t : 128 * t + 128, :] = work[t].T
 
-def finish_kernel(nb, gram, first, between, states, projected, lower, inverse, work):
-    factor_kernel(nb, gram, lower, inverse, work)
+def near_identity_kernel(gram, inverse):
+    size = gram.shape[0]
+    row = lax.broadcasted_iota(jnp.int32, (size, size), 0)
+    col = lax.broadcasted_iota(jnp.int32, (size, size), 1)
+    ident = jnp.where(row == col, 1.0, 0.0)
+    weight = jnp.where(row > col, 1.0, 0.5 * ident)
+
+    def times(left, right, across):
+        return lax.dot_general(
+            left, right, (((1,), (across,)), ((), ())),
+            precision=HIGHEST, preferred_element_type=jnp.float32,
+        )
+
+    error = gram[...] - ident
+    shift = None
+    for step in range(NEAR_STEPS):
+        low = weight * error
+        shift = low if shift is None else shift + low - times(low, shift, 0)
+        if step < NEAR_STEPS - 1:
+            cross = times(low, error, 0)
+            error = times(low + cross, low, 1) - cross - cross.T
+    inverse[...] = ident - shift
+    return jnp.sum(error * error)
+
+
+def finish_kernel(
+    nb, gram, first, between, lower_one, states, projected, factor, lower, inverse, work
+):
+    factor[...] = lower_one[...]
+    left = near_identity_kernel(gram, inverse)
+
+    @pl.when(jnp.logical_not(left < NEAR_LEFT * NEAR_LEFT))
+    def _():
+        factor_kernel(nb, gram, lower, inverse, work)
+
     states[...] = rotated(first[...], inverse[...])
     half = rotated(between[...], inverse[...])
     projected[...] = jnp.dot(
@@ -700,24 +736,23 @@
         1,
         pltpu.HBM,
     )
-    lower_one, inverse_one = local_call(
-        functools.partial(factor_kernel, PANEL), [gram_one], [square, square], [work]
-    )
-    first, gram_two, between = call(
+    first, gram_two, between, lower_one = call(
         functools.partial(rotate_kernel, dims, sites),
-        [flat, image, inverse_one],
+        [flat, image, gram_one],
         [],
+        [(count, columns), square, square, square],
+        [pltpu.VMEM(square, jnp.float32), work, pltpu.VMEM((count, columns), jnp.float32)]
+        + sums
+        + sums,
+        2,
+    )
+    states, projected, factor = local_call(
+        functools.partial(finish_kernel, PANEL),
+        [gram_two, first, between, lower_one],
         [(count, columns), square, square],
-        [pltpu.VMEM((count, columns), jnp.float32)] + sums + sums,
-        2,
-    )
-    states, projected = local_call(
-        functools.partial(finish_kernel, PANEL),
-        [gram_two, first, between],
-        [(count, columns), square],
         [pltpu.VMEM(square, jnp.float32), pltpu.VMEM(square, jnp.float32), work],
     )
-    return (states.reshape(shape), projected, lower_one)
+    return (states.reshape(shape), projected, factor)
 
 
 def solution(mesh):

time: 116 us -> 108 us (0.931)
  Pallas kernels: 113 us -> 104 us
    pallas_call x2 -> x1, Pallas kernels: 21.6 us -> 5.47 us  [local_call(): pl.pallas_call(kernel, out_shape=[jax.ShapeDtypeStruct(shape, jnp.float32...]
    pallas_call x2, Pallas kernels: 91 us -> 99 us  [call(): pl.pallas_call(kernel, out_shape=[jax.ShapeDtypeStruct(shape, jnp.float32...]
where the time goes in v6:
time: 108 us
  Pallas kernels  104 us (96%)
  local copies, waits for them, and re-layouts  1.8 us (2%)
  between operations  1.33 us (1%)
    pallas_call x2, Pallas kernels, call(): pl.pallas_call(kernel, out_shape=[jax.ShapeDtypeStruct(shape, jnp.float32...  99 us
    pallas_call x1, Pallas kernels, local_call(): pl.pallas_call(kernel, out_shape=[jax.ShapeDtypeStruct(shape, jnp.float32...  5.47 us

profile of v6, /device:TPU:1, one launch (start us, length us, event | category | flops | bytes accessed | tf_op | source)
XLA Modules:
  0.0 107.6 jit_solution(520805679970670645)
XLA Ops:
  0.6 0.0 copy-start.2
  1.3 0.0 copy-done.2
  1.3 0.0 copy-start
  1.3 1.0 copy-done
  2.4 0.0 copy-start.1
  2.4 0.8 copy-done.1
  3.1 67.0 %shard_map.67 = (f32[512,256]{1,0:T(8,128)S(1)}, f32[512,256]{1,0:T(8,128)S(1)}, f32[256,256]{1,0:T(8,128)S(1)}) custom-call(f32[8,8,8,256]{3,2,1,0:T(8,128)S(1)} %copy-done, f32[8,8,8]{2,1,0:T(8,128)S(1)} %copy-done.1, f32[13]{0:T(128)S(1)} %copy-done.2, f32[1]{0:T(128)S(6)} %copy.7.cut_frac), custom_call_target="tpu_custom_call" | custom-call | tf_op jit(solution)/shard_map/pallas_call | solution.py:558
  70.1 32.0 %shard_map.68 = (f32[512,256]{1,0:T(8,128)S(1)}, f32[256,256]{1,0:T(8,128)S(1)}, f32[256,256]{1,0:T(8,128)S(1)}, f32[256,256]{1,0:T(8,128)S(1)}) custom-call(f32[512,256]{1,0:T(8,128)S(1)} %get-tuple-element.13.flat, f32[512,256]{1,0:T(8,128)S(1)} %get-tuple-element.14.image, f32[256,256]{1,0:T(8,128)S(1)} %get-tuple-element.15.gram_one), custom_call_target="tpu_custom_call" | custom-call | tf_op jit(solution)/shard_map/pallas_call | solution.py:558
  102.1 5.5 %shard_map.69 = (f32[512,256]{1,0:T(8,128)}, f32[256,256]{1,0:T(8,128)}, f32[256,256]{1,0:T(8,128)}) custom-call(f32[256,256]{1,0:T(8,128)S(1)} %get-tuple-element.16.gram, f32[512,256]{1,0:T(8,128)S(1)} %get-tuple-element.17.first, f32[256,256]{1,0:T(8,128)S(1)} %get-tuple-element.18.between, f32[256,256]{1,0:T(8,128)S(1)} %get-tuple-element.19.lower_one), custom_call_target="tpu_custom_call" | custom-call | tf_op jit(solution)/shard_map/pallas_call | solution.py:699
Async XLA Ops:
  0.6 0.7 copy-start.2
  1.3 1.0 copy-start
  2.4 0.8 copy-start.1

commit v7 on v6

--- a/solution.py
+++ b/solution.py
@@ -400,7 +400,12 @@
         sigma = sigma_next
 
 
-def filter_kernel(dims, shape, sites, block, onsite, hopping, cut_frac, flat, image, gram, *scratch):
+def filter_kernel(
+    dims, shape, sites,
+    block, onsite, hopping, cut_frac,
+    first, gram_two, between, lower,
+    *scratch,
+):
     size_x, size_y, size_z, lanes = shape
     per_half = HALO_REFS
     halves = []
@@ -410,7 +415,8 @@
     (
         onsite_here, levels, input_sems,
         max_plane, max_column, max_sems, coef,
-        local, total, plane_buf, column_buf, sums_sems,
+        flat, image, moved, gram, inverse, work,
+        *sum_refs,
     ) = scratch[HALVES * per_half :]
     enter(dims, True)
     copies = [pltpu.make_async_copy(onsite, onsite_here, input_sems.at[HALVES])]
@@ -475,8 +481,11 @@
             pack_corners(shape, after, field, corner_out)
             halo_send(dims, shape, after, refs, sems)
     slot = DEG % 2
-    sums = AllReduce(dims, local, total, plane_buf, column_buf, sums_sems)
-    local[...] = product(flat[...], flat[...])
+    per_sum = len(sum_refs) // 3
+    sums, sums_two, sums_between = [
+        AllReduce(dims, *sum_refs[k * per_sum : (k + 1) * per_sum]) for k in range(3)
+    ]
+    sums.local[...] = product(flat[...], flat[...])
     sums.scatter()
     for refs, shifted, sems in halves:
         halo_wait(dims, shape, slot, refs, sems, True)
@@ -495,7 +504,11 @@
         halo_wait(dims, shape, 1 - slot, refs, sems, False)
         halo_wait(dims, shape, slot, refs, sems, False)
     sums.finish()
-    gram[...] = total[...] / sites
+    gram[...] = sums.total[...] / sites
+    factor_kernel(PANEL, gram, lower, inverse, work)
+    rotate_and_sum(
+        dims, sites, flat, image, inverse, first, gram_two, between, moved, sums_two, sums_between
+    )
 
 
 def site_rows(shape, x, y):
@@ -523,33 +536,21 @@
     )
 
 
-def rotate_kernel(
-    dims, sites,
-    flat, image, gram_one,
-    first, gram, between, lower,
-    factor, work, moved,
-    local, total, plane_buf, column_buf, sums_sems,
-    local_b, total_b, plane_buf_b, column_buf_b, sums_sems_b,
-):
-    enter(dims, False)
-    sums = AllReduce(dims, local, total, plane_buf, column_buf, sums_sems)
-    sums_b = AllReduce(dims, local_b, total_b, plane_buf_b, column_buf_b, sums_sems_b)
-    factor_kernel(PANEL, gram_one, lower, factor, work)
-    first[...] = rotated(flat[...], factor[...])
-    local[...] = product(first[...], first[...])
-    entered(dims, False)
+def rotate_and_sum(dims, sites, flat, image, inverse, first, gram, between, moved, sums, sums_b):
+    first[...] = rotated(flat[...], inverse[...])
+    sums.local[...] = product(first[...], first[...])
     sums.scatter()
-    moved[...] = rotated(image[...], factor[...])
-    local_b[...] = product(first[...], moved[...])
+    moved[...] = rotated(image[...], inverse[...])
+    sums_b.local[...] = product(first[...], moved[...])
     sums_b.scatter()
     sums.across()
     sums_b.across()
     sums.gather()
     sums_b.gather()
     sums.finish()
-    gram[...] = total[...] / sites
+    gram[...] = sums.total[...] / sites
     sums_b.finish()
-    between[...] = total_b[...] / sites
+    between[...] = sums_b.total[...] / sites
 
 
 def call(kernel, inputs, scalars, outputs, scratch, ident, space=pltpu.VMEM):
@@ -717,11 +718,11 @@
     work = pltpu.VMEM((2 * (columns // 128), columns, 128), jnp.float32)
     lanes = columns // HALVES
     part = (size_x, size_y, size_z, lanes)
-    flat, image, gram_one = call(
+    first, gram_two, between, lower_one = call(
         functools.partial(filter_kernel, dims, part, sites),
-        [block, onsite],
+        [pltpu.with_memory_space_constraint(v, pltpu.HBM) for v in (block, onsite)],
         [hopping, cut_frac],
-        [(count, columns), (count, columns), square],
+        [(count, columns), square, square, square],
         halo_scratch(part, 2) * HALVES
         + [
             pltpu.VMEM((size_x, size_y, size_z), jnp.float32),
@@ -732,19 +733,12 @@
             pltpu.SemaphoreType.DMA((4,)),
             pltpu.VMEM((2 * DEG, 8, 128), jnp.float32),
         ]
-        + sums,
+        + [pltpu.VMEM((count, columns), jnp.float32)] * 3
+        + [pltpu.VMEM(square, jnp.float32)] * 2
+        + [work]
+        + sums * 3,
         1,
         pltpu.HBM,
-    )
-    first, gram_two, between, lower_one = call(
-        functools.partial(rotate_kernel, dims, sites),
-        [flat, image, gram_one],
-        [],
-        [(count, columns), square, square, square],
-        [pltpu.VMEM(square, jnp.float32), work, pltpu.VMEM((count, columns), jnp.float32)]
-        + sums
-        + sums,
-        2,
     )
     states, projected, factor = local_call(
         functools.partial(finish_kernel, PANEL),

time: 108 us -> 104 us (0.963)
  local copies, waits for them, and re-layouts: 1.8 us -> 0.01 us
    unnamed x6 -> x2, local copies, waits for them, and re-layouts: 1.8 us -> 0.01 us
    pallas_call x2 -> x1, Pallas kernels: 99 us -> 97.2 us  [call(): pl.pallas_call(kernel, out_shape=[jax.ShapeDtypeStruct(shape, jnp.float32...]
where the time goes in v7:
time: 104 us
  Pallas kernels  103 us (99%)
  between operations  1.31 us (1%)
    pallas_call x1, Pallas kernels, call(): pl.pallas_call(kernel, out_shape=[jax.ShapeDtypeStruct(shape, jnp.float32...  97.2 us
    pallas_call x1, Pallas kernels, local_call(): pl.pallas_call(kernel, out_shape=[jax.ShapeDtypeStruct(shape, jnp.float32...  5.47 us

profile of v7, /device:TPU:1, one launch (start us, length us, event | category | flops | bytes accessed | tf_op | source)
XLA Modules:
  0.0 104.0 jit_solution(13440916733887470043)
XLA Ops:
  0.6 0.0 copy-start
  1.3 0.0 copy-done
  1.3 97.2 %shard_map.67 = (f32[512,256]{1,0:T(8,128)S(1)}, f32[256,256]{1,0:T(8,128)S(1)}, f32[256,256]{1,0:T(8,128)S(1)}, f32[256,256]{1,0:T(8,128)S(1)}) custom-call(f32[8,8,8,256]{3,2,1,0:T(8,128)} %block.1, f32[8,8,8]{2,1,0:T(8,128)} %onsite.1, f32[13]{0:T(128)S(1)} %copy-done, f32[1]{0:T(128)S(6)} %copy.7.cut_frac), custom_call_target="tpu_custom_call" | custom-call | tf_op jit(solution)/shard_map/pallas_call | solution.py:559
  98.6 5.5 %shard_map.68 = (f32[512,256]{1,0:T(8,128)}, f32[256,256]{1,0:T(8,128)}, f32[256,256]{1,0:T(8,128)}) custom-call(f32[256,256]{1,0:T(8,128)S(1)} %get-tuple-element.10.gram, f32[512,256]{1,0:T(8,128)S(1)} %get-tuple-element.11.first, f32[256,256]{1,0:T(8,128)S(1)} %get-tuple-element.12.between, f32[256,256]{1,0:T(8,128)S(1)} %get-tuple-element.13.lower_one), custom_call_target="tpu_custom_call" | custom-call | tf_op jit(solution)/shard_map/pallas_call | solution.py:700
Async XLA Ops:
  0.6 0.7 copy-start

commit v8 on v7

--- a/solution.py
+++ b/solution.py
@@ -419,6 +419,7 @@
         *sum_refs,
     ) = scratch[HALVES * per_half :]
     enter(dims, True)
+    early = moved
     copies = [pltpu.make_async_copy(onsite, onsite_here, input_sems.at[HALVES])]
     for half, (refs, _, _) in enumerate(halves):
         inside = refs[0].at[0, pl.ds(1, size_x), pl.ds(1, size_y)]
@@ -447,14 +448,13 @@
         halo_send(dims, shape, 0, refs, sems)
         if index == 0:
             max_start(dims, None, max_plane, max_sems)
-    max_middle(dims, max_plane, max_column, max_sems)
     for step in range(DEG):
         slot, after = step % 2, (step + 1) % 2
         for half, (refs, shifted, sems) in enumerate(halves):
             field, face, edge, corner, face_out, edge_out, corner_out = refs
             halo_wait(dims, shape, slot, refs, sems, True)
             shift_columns(shape, slot, field, face, edge, corner, shifted)
-            if step == 0 and half == 0:
+            if step == 1 and half == 0:
                 reach = jnp.abs(hopping[0])
                 for k in range(1, len(POSITIVE)):
                     reach = reach + jnp.abs(hopping[k])
@@ -467,19 +467,28 @@
             def _(x):
                 totals, centres = apply_rows(shape, slot, x, field, shifted, levels, hopping)
                 for y in range(size_y):
-                    value = totals[y] - coef[0] * centres[y]
-                    if step == 0:
-                        value = coef[1] * value
-                    else:
+                    mine = (site_rows(shape, x, y), slice(lanes * half, lanes * (half + 1)))
+                    value = totals[y]
+                    if step == 1:
                         older = field[after, x + 1, y + 1]
-                        value = coef[2 * step] * value - coef[2 * step + 1] * older
+                        newer = coef[1] * (centres[y] - coef[0] * older)
+                        early[mine] = newer
+                        value = coef[1] * (value - coef[0] * centres[y])
+                    elif step > 1:
+                        newer = centres[y]
+                        older = early[mine] if step == 2 else field[after, x + 1, y + 1]
+                    if step:
+                        value = coef[2 * step] * (value - coef[0] * newer)
+                        value = value - coef[2 * step + 1] * older
                     if step == DEG - 1:
-                        flat[site_rows(shape, x, y), lanes * half : lanes * (half + 1)] = value
+                        flat[mine] = value
                     field[after, x + 1, y + 1] = value
                     pack_column(shape, after, x, y, value, face_out, edge_out)
 
             pack_corners(shape, after, field, corner_out)
             halo_send(dims, shape, after, refs, sems)
+            if step == 0 and half == 0:
+                max_middle(dims, max_plane, max_column, max_sems)
     slot = DEG % 2
     per_sum = len(sum_refs) // 3
     sums, sums_two, sums_between = [
@@ -626,15 +635,18 @@
         if stop < size:
             full = {t: jnp.concatenate(panel[t], 0) if groups > 1 else panel[t][0] for t in active}
             recips = jnp.concatenate(recip, 0) if groups > 1 else recip[0]
-            for u in range(tiles):
-                low = max(128 * u, stop)
-                if low >= 128 * (u + 1):
+            chunks = [(stop, stop + nb)] + [
+                (max(128 * u, stop + nb), 128 * (u + 1)) for u in range(tiles)
+            ]
+            for low, high in chunks:
+                if low >= high:
                     continue
-                left = (full[u] * recips)[:, low - 128 * u :]
+                u = low // 128
+                left = (full[u] * recips)[:, low - 128 * u : high - 128 * u]
                 for t in active:
                     if t < u:
                         continue
-                    work[t, low : 128 * (u + 1)] -= lax.dot_general(
+                    work[t, low:high] -= lax.dot_general(
                         left, full[t], (((0,), (0,)), ((), ())),
                         precision=HIGHEST, preferred_element_type=jnp.float32)
         for g in range(groups):

time: 104 us -> 99.8 us (0.960)
  Pallas kernels: 103 us -> 98.3 us
    pallas_call x1, Pallas kernels: 97.2 us -> 92.9 us  [call(): pl.pallas_call(kernel, out_shape=[jax.ShapeDtypeStruct(shape, jnp.float32...]
where the time goes in v8:
time: 99.8 us; the launch traced here: 99.6 us
  Pallas kernels  98.3 us (98%)
  between operations  1.31 us (1%)
    pallas_call x1, Pallas kernels, call(): pl.pallas_call(kernel, out_shape=[jax.ShapeDtypeStruct(shape, jnp.float32...  92.9 us
    pallas_call x1, Pallas kernels, local_call(): pl.pallas_call(kernel, out_shape=[jax.ShapeDtypeStruct(shape, jnp.float32...  5.47 us

profile of v8, /device:TPU:1, one launch (start us, length us, event | category | flops | bytes accessed | tf_op | source)
XLA Modules:
  0.0 99.6 jit_solution(11377760876123934982)
XLA Ops:
  0.6 0.0 copy-start
  1.3 0.0 copy-done
  1.3 92.9 %shard_map.67 = (f32[512,256]{1,0:T(8,128)S(1)}, f32[256,256]{1,0:T(8,128)S(1)}, f32[256,256]{1,0:T(8,128)S(1)}, f32[256,256]{1,0:T(8,128)S(1)}) custom-call(f32[8,8,8,256]{3,2,1,0:T(8,128)} %block.1, f32[8,8,8]{2,1,0:T(8,128)} %onsite.1, f32[13]{0:T(128)S(1)} %copy-done, f32[1]{0:T(128)S(6)} %copy.7.cut_frac), custom_call_target="tpu_custom_call" | custom-call | tf_op jit(solution)/shard_map/pallas_call | solution.py:568
  94.2 5.5 %shard_map.68 = (f32[512,256]{1,0:T(8,128)}, f32[256,256]{1,0:T(8,128)}, f32[256,256]{1,0:T(8,128)}) custom-call(f32[256,256]{1,0:T(8,128)S(1)} %get-tuple-element.10.gram, f32[512,256]{1,0:T(8,128)S(1)} %get-tuple-element.11.first, f32[256,256]{1,0:T(8,128)S(1)} %get-tuple-element.12.between, f32[256,256]{1,0:T(8,128)S(1)} %get-tuple-element.13.lower_one), custom_call_target="tpu_custom_call" | custom-call | tf_op jit(solution)/shard_map/pallas_call | solution.py:712
Async XLA Ops:
  0.6 0.7 copy-start

commit v9 on v8

--- a/solution.py
+++ b/solution.py
@@ -171,7 +171,7 @@
     ]
 
 
-def max_start(dims, value, plane_buf, sems):
+def max_start(dims, plane_buf, sems):
     plane = dims[0] * dims[2]
     place = lax.axis_index("gx") * dims[2] + lax.axis_index("gz")
 
@@ -418,7 +418,6 @@
         flat, image, moved, gram, inverse, work,
         *sum_refs,
     ) = scratch[HALVES * per_half :]
-    enter(dims, True)
     early = moved
     copies = [pltpu.make_async_copy(onsite, onsite_here, input_sems.at[HALVES])]
     for half, (refs, _, _) in enumerate(halves):
@@ -427,11 +426,7 @@
         copies.append(pltpu.make_async_copy(source, inside, input_sems.at[half]))
     for copy in copies:
         copy.start()
-    for refs, _, _ in halves:
-        zero_border(dims, shape, 2, *refs[:4])
-    copies[0].wait()
-    place = place_of(dims)
-    max_plane[place] = jnp.full((8, 128), jnp.max(jnp.abs(onsite_here[...])), jnp.float32)
+    enter(dims, True)
     for copy, (refs, _, _) in zip(copies[1:], halves):
         copy.wait()
         field, face_out, edge_out, corner_out = refs[0], *refs[4:]
@@ -442,12 +437,16 @@
                 pack_column(shape, 0, x, y, field[0, x + 1, y + 1], face_out, edge_out)
 
         pack_corners(shape, 0, field, corner_out)
+    copies[0].wait()
+    place = place_of(dims)
+    max_plane[place] = jnp.full((8, 128), jnp.max(jnp.abs(onsite_here[...])), jnp.float32)
+    entered(dims, True)
+    for refs, _, sems in halves:
+        halo_send(dims, shape, 0, refs, sems)
+    max_start(dims, max_plane, max_sems)
+    for refs, _, _ in halves:
+        zero_border(dims, shape, 2, *refs[:4])
     spread(onsite_here, levels)
-    entered(dims, True)
-    for index, (refs, _, sems) in enumerate(halves):
-        halo_send(dims, shape, 0, refs, sems)
-        if index == 0:
-            max_start(dims, None, max_plane, max_sems)
     for step in range(DEG):
         slot, after = step % 2, (step + 1) % 2
         for half, (refs, shifted, sems) in enumerate(halves):
@@ -460,8 +459,6 @@
                     reach = reach + jnp.abs(hopping[k])
                 bound = max_end(dims, max_plane, max_column, max_sems) + 2.0 * reach
                 filter_coefficients(bound, cut_frac[0], coef)
-            if step:
-                halo_wait(dims, shape, after, refs, sems, False)
 
             @pl.loop(0, size_x)
             def _(x):
@@ -487,6 +484,7 @@
 
             pack_corners(shape, after, field, corner_out)
             halo_send(dims, shape, after, refs, sems)
+            halo_wait(dims, shape, slot, refs, sems, False)
             if step == 0 and half == 0:
                 max_middle(dims, max_plane, max_column, max_sems)
     slot = DEG % 2
@@ -510,7 +508,6 @@
 
     sums.gather()
     for refs, _, sems in halves:
-        halo_wait(dims, shape, 1 - slot, refs, sems, False)
         halo_wait(dims, shape, slot, refs, sems, False)
     sums.finish()
     gram[...] = sums.total[...] / sites

time: 99.8 us -> 99.3 us (level)
  no operation moved by 1% of the time
where the time goes in v9:
time: 99.3 us; the launch traced here: 99.2 us
  Pallas kernels  97.9 us (99%)
  between operations  1.31 us (1%)
    pallas_call x1, Pallas kernels, call(): pl.pallas_call(kernel, out_shape=[jax.ShapeDtypeStruct(shape, jnp.float32...  92.4 us
    pallas_call x1, Pallas kernels, local_call(): pl.pallas_call(kernel, out_shape=[jax.ShapeDtypeStruct(shape, jnp.float32...  5.47 us

profile of v9, /device:TPU:1, one launch (start us, length us, event | category | flops | bytes accessed | tf_op | source)
XLA Modules:
  0.0 99.2 jit_solution(12705223227638237422)
XLA Ops:
  0.6 0.0 copy-start
  1.3 0.0 copy-done
  1.3 92.4 %shard_map.67 = (f32[512,256]{1,0:T(8,128)S(1)}, f32[256,256]{1,0:T(8,128)S(1)}, f32[256,256]{1,0:T(8,128)S(1)}, f32[256,256]{1,0:T(8,128)S(1)}) custom-call(f32[8,8,8,256]{3,2,1,0:T(8,128)} %block.1, f32[8,8,8]{2,1,0:T(8,128)} %onsite.1, f32[13]{0:T(128)S(1)} %copy-done, f32[1]{0:T(128)S(6)} %copy.7.cut_frac), custom_call_target="tpu_custom_call" | custom-call | tf_op jit(solution)/shard_map/pallas_call | solution.py:565
  93.7 5.5 %shard_map.68 = (f32[512,256]{1,0:T(8,128)}, f32[256,256]{1,0:T(8,128)}, f32[256,256]{1,0:T(8,128)}) custom-call(f32[256,256]{1,0:T(8,128)S(1)} %get-tuple-element.10.gram, f32[512,256]{1,0:T(8,128)S(1)} %get-tuple-element.11.first, f32[256,256]{1,0:T(8,128)S(1)} %get-tuple-element.12.between, f32[256,256]{1,0:T(8,128)S(1)} %get-tuple-element.13.lower_one), custom_call_target="tpu_custom_call" | custom-call | tf_op jit(solution)/shard_map/pallas_call | solution.py:709
Async XLA Ops:
  0.6 0.7 copy-start

commit v10 on v9

--- a/solution.py
+++ b/solution.py
@@ -329,10 +329,19 @@
         shifted[0, x, y] = jnp.where(place == 0, below, pltpu.roll(value, 1, 0))
         shifted[1, x, y] = jnp.where(place == size_z - 1, above, pltpu.roll(value, size_z - 1, 0))
 
-    @pl.loop(0, size_x + 2)
+    def row(x, y):
+        return face[slot, 0, x, y : y + 1], face[slot, 1, x, y : y + 1]
+
+    for x in (0, size_x + 1):
+        for y in range(size_y):
+            put(x, y + 1, *row(x, y))
+
+    @pl.loop(1, size_x + 1)
     def _(x):
         for y in range(size_y):
-            put(x, y + 1, face[slot, 0, x, y : y + 1], face[slot, 1, x, y : y + 1])
+            below, above = row(x, y)
+            shifted[0, x, y + 1, 0:1] = below
+            shifted[1, x, y + 1, size_z - 1 : size_z] = above
 
     for far in (0, 1):
         y = size_y + 1 if far else 0
@@ -344,6 +353,17 @@
         for right in (0, 1):
             x = size_x + 1 if right else 0
             put(x, y, corner[slot, 0, far, right], corner[slot, 1, far, right])
+
+
+def shift_inside(shape, slot, field, shifted):
+    size_x, size_y, size_z, _ = shape
+
+    @pl.loop(1, size_x + 1)
+    def _(x):
+        for y in range(1, size_y + 1):
+            value = field[slot, x, y]
+            shifted[0, x, y] = pltpu.roll(value, 1, 0)
+            shifted[1, x, y] = pltpu.roll(value, size_z - 1, 0)
 
 
 def apply_rows(shape, slot, x, field, shifted, onsite, hopping):
@@ -444,8 +464,9 @@
     for refs, _, sems in halves:
         halo_send(dims, shape, 0, refs, sems)
     max_start(dims, max_plane, max_sems)
-    for refs, _, _ in halves:
+    for refs, shifted, _ in halves:
         zero_border(dims, shape, 2, *refs[:4])
+        shift_inside(shape, 0, refs[0], shifted)
     spread(onsite_here, levels)
     for step in range(DEG):
         slot, after = step % 2, (step + 1) % 2
@@ -484,6 +505,7 @@
 
             pack_corners(shape, after, field, corner_out)
             halo_send(dims, shape, after, refs, sems)
+            shift_inside(shape, after, field, shifted)
             halo_wait(dims, shape, slot, refs, sems, False)
             if step == 0 and half == 0:
                 max_middle(dims, max_plane, max_column, max_sems)

time: 99.3 us -> 99.3 us (level)
  no operation moved by 1% of the time
where the time goes in v10:
time: 99.3 us
  Pallas kernels  97.9 us (99%)
  between operations  1.31 us (1%)
    pallas_call x1, Pallas kernels, call(): pl.pallas_call(kernel, out_shape=[jax.ShapeDtypeStruct(shape, jnp.float32...  92.5 us
    pallas_call x1, Pallas kernels, local_call(): pl.pallas_call(kernel, out_shape=[jax.ShapeDtypeStruct(shape, jnp.float32...  5.47 us

profile of v10, /device:TPU:1, one launch (start us, length us, event | category | flops | bytes accessed | tf_op | source)
XLA Modules:
  0.0 99.3 jit_solution(5245456973997238269)
XLA Ops:
  0.6 0.0 copy-start
  1.3 0.0 copy-done
  1.3 92.5 %shard_map.67 = (f32[512,256]{1,0:T(8,128)S(1)}, f32[256,256]{1,0:T(8,128)S(1)}, f32[256,256]{1,0:T(8,128)S(1)}, f32[256,256]{1,0:T(8,128)S(1)}) custom-call(f32[8,8,8,256]{3,2,1,0:T(8,128)} %block.1, f32[8,8,8]{2,1,0:T(8,128)} %onsite.1, f32[13]{0:T(128)S(1)} %copy-done, f32[1]{0:T(128)S(6)} %copy.7.cut_frac), custom_call_target="tpu_custom_call" | custom-call | tf_op jit(solution)/shard_map/pallas_call | solution.py:587
  93.8 5.5 %shard_map.68 = (f32[512,256]{1,0:T(8,128)}, f32[256,256]{1,0:T(8,128)}, f32[256,256]{1,0:T(8,128)}) custom-call(f32[256,256]{1,0:T(8,128)S(1)} %get-tuple-element.10.gram, f32[512,256]{1,0:T(8,128)S(1)} %get-tuple-element.11.first, f32[256,256]{1,0:T(8,128)S(1)} %get-tuple-element.12.between, f32[256,256]{1,0:T(8,128)S(1)} %get-tuple-element.13.lower_one), custom_call_target="tpu_custom_call" | custom-call | tf_op jit(solution)/shard_map/pallas_call | solution.py:731
Async XLA Ops:
  0.6 0.7 copy-start

commit v11 on v9

--- a/solution.py
+++ b/solution.py
@@ -37,6 +37,28 @@
     return peer, {"gx": peer // size_z, "gz": lax.rem(peer, size_z)}
 
 
+def bits(value, count):
+    return [lax.rem(value // (1 << k), 2) for k in range(count)]
+
+
+def plane_order(dims):
+    hops = (0, 1, 2, 1)
+    flips = [(a, b) for a in range(dims[0]) for b in range(dims[2]) if (a, b) != (0, 0)]
+    return sorted(flips, key=lambda f: -hops[f[1] % 4] - hops[f[1] // 4 * 2 + f[0] // 2])
+
+
+def plane_peers(dims):
+    bits_x, bits_z = [bits(lax.axis_index(axis), size.bit_length() - 1)
+                      for axis, size in (("gx", dims[0]), ("gz", dims[2]))]
+
+    def flipped(values, mask):
+        return sum((1 - v if mask >> k & 1 else v) * (1 << k) for k, v in enumerate(values))
+
+    for a, b in plane_order(dims):
+        gx, gz = flipped(bits_x, a), flipped(bits_z, b)
+        yield gx * dims[2] + gz, {"gx": gx, "gz": gz}
+
+
 def column_peer(dims, offset):
     peer = lax.rem(lax.axis_index("gy") + offset, dims[1])
     return peer, {"gy": peer}
@@ -116,12 +138,10 @@
         self.mine = pl.ds(pl.multiple_of(place_of(dims) * self.rows, self.rows), self.rows)
 
     def scatter(self):
-        @pl.loop(1, self.plane)
-        def _(k):
-            peer, device = plane_peer(self.dims, k)
+        for k, (peer, device) in enumerate(plane_peers(self.dims)):
             theirs = pl.ds(pl.multiple_of(peer * self.rows, self.rows), self.rows)
             send(
-                self.local.at[theirs], self.plane_buf.at[k - 1],
+                self.local.at[theirs], self.plane_buf.at[k],
                 self.sems.at[0], self.sems.at[1], device,
             )
 
@@ -132,9 +152,7 @@
             0, self.plane - 1, lambda k, acc: acc + self.plane_buf[k], self.local[self.mine]
         )
         mine = self.column_buf.at[level]
-
-        @pl.loop(1, self.column)
-        def _(k):
+        for k in sorted(range(1, self.column), key=lambda k: -min(k, self.column - k)):
             _, device = column_peer(self.dims, k)
             send(mine, mine, self.sems.at[2], self.sems.at[3], device)
 
@@ -146,9 +164,7 @@
         self.total[self.mine] = part
         mine = self.total.at[self.mine]
 
-        @pl.loop(1, self.plane)
-        def _(k):
-            _, device = plane_peer(self.dims, k)
+        for _, device in plane_peers(self.dims):
             send(mine, mine, self.sems.at[4], self.sems.at[5], device)
 
     def finish(self):

time: 99.3 us -> 98.2 us (0.989)
  Pallas kernels: 97.9 us -> 96.8 us
    pallas_call x1, Pallas kernels: 92.4 us -> 91.3 us  [call(): pl.pallas_call(kernel, out_shape=[jax.ShapeDtypeStruct(shape, jnp.float32...]
where the time goes in v11:
time: 98.2 us; the launch traced here: 98.1 us
  Pallas kernels  96.8 us (99%)
  between operations  1.31 us (1%)
    pallas_call x1, Pallas kernels, call(): pl.pallas_call(kernel, out_shape=[jax.ShapeDtypeStruct(shape, jnp.float32...  91.3 us
    pallas_call x1, Pallas kernels, local_call(): pl.pallas_call(kernel, out_shape=[jax.ShapeDtypeStruct(shape, jnp.float32...  5.48 us

profile of v11, /device:TPU:1, one launch (start us, length us, event | category | flops | bytes accessed | tf_op | source)
XLA Modules:
  0.0 98.1 jit_solution(3096377213595632038)
XLA Ops:
  0.6 0.0 copy-start
  1.3 0.0 copy-done
  1.3 91.3 %shard_map.67 = (f32[512,256]{1,0:T(8,128)S(1)}, f32[256,256]{1,0:T(8,128)S(1)}, f32[256,256]{1,0:T(8,128)S(1)}, f32[256,256]{1,0:T(8,128)S(1)}) custom-call(f32[8,8,8,256]{3,2,1,0:T(8,128)} %block.1, f32[8,8,8]{2,1,0:T(8,128)} %onsite.1, f32[13]{0:T(128)S(1)} %copy-done, f32[1]{0:T(128)S(6)} %copy.7.cut_frac), custom_call_target="tpu_custom_call" | custom-call | tf_op jit(solution)/shard_map/pallas_call | solution.py:581
  92.6 5.5 %shard_map.68 = (f32[512,256]{1,0:T(8,128)}, f32[256,256]{1,0:T(8,128)}, f32[256,256]{1,0:T(8,128)}) custom-call(f32[256,256]{1,0:T(8,128)S(1)} %get-tuple-element.10.gram, f32[512,256]{1,0:T(8,128)S(1)} %get-tuple-element.11.first, f32[256,256]{1,0:T(8,128)S(1)} %get-tuple-element.12.between, f32[256,256]{1,0:T(8,128)S(1)} %get-tuple-element.13.lower_one), custom_call_target="tpu_custom_call" | custom-call | tf_op jit(solution)/shard_map/pallas_call | solution.py:725
Async XLA Ops:
  0.6 0.7 copy-start

commit v12 on v11

--- a/solution.py
+++ b/solution.py
@@ -81,22 +81,20 @@
 def enter(dims, halo):
     barrier = pltpu.get_barrier_semaphore()
 
-    @pl.loop(1, dims[0] * dims[2])
-    def _(k):
-        pl.semaphore_signal(barrier, inc=1, device_id=plane_peer(dims, k)[1], device_id_type=MESH)
-
-    @pl.loop(1, dims[1])
-    def _(k):
-        pl.semaphore_signal(barrier, inc=1, device_id=column_peer(dims, k)[1], device_id_type=MESH)
+    def tell(device):
+        pl.semaphore_signal(barrier, inc=1, device_id=device, device_id_type=MESH)
 
     if halo:
-        for offset in OFFSETS:
+        for offset in sorted(OFFSETS, key=lambda d: -3 * abs(d[2]) - abs(d[1]) - abs(d[0])):
 
             @pl.when(has_neighbour(dims, offset))
             def _():
-                pl.semaphore_signal(
-                    barrier, inc=1, device_id=neighbour(offset), device_id_type=MESH
-                )
+                tell(neighbour(offset))
+
+    for k in sorted(range(1, dims[1]), key=lambda k: -min(k, dims[1] - k)):
+        tell(column_peer(dims, k)[1])
+    for _, device in plane_peers(dims):
+        tell(device)
 
 
 def entered(dims, halo):

time: 98.2 us -> 96.9 us (0.987)
  Pallas kernels: 96.8 us -> 95.5 us
    pallas_call x1, Pallas kernels: 91.3 us -> 90 us  [call(): pl.pallas_call(kernel, out_shape=[jax.ShapeDtypeStruct(shape, jnp.float32...]
where the time goes in v12:
time: 96.9 us; the launch traced here: 96.8 us
  Pallas kernels  95.5 us (99%)
  between operations  1.31 us (1%)
    pallas_call x1, Pallas kernels, call(): pl.pallas_call(kernel, out_shape=[jax.ShapeDtypeStruct(shape, jnp.float32...  90 us
    pallas_call x1, Pallas kernels, local_call(): pl.pallas_call(kernel, out_shape=[jax.ShapeDtypeStruct(shape, jnp.float32...  5.47 us

profile of v12, /device:TPU:1, one launch (start us, length us, event | category | flops | bytes accessed | tf_op | source)
XLA Modules:
  0.0 96.8 jit_solution(1531545229976808123)
XLA Ops:
  0.6 0.0 copy-start
  1.3 0.0 copy-done
  1.3 90.0 %shard_map.67 = (f32[512,256]{1,0:T(8,128)S(1)}, f32[256,256]{1,0:T(8,128)S(1)}, f32[256,256]{1,0:T(8,128)S(1)}, f32[256,256]{1,0:T(8,128)S(1)}) custom-call(f32[8,8,8,256]{3,2,1,0:T(8,128)} %block.1, f32[8,8,8]{2,1,0:T(8,128)} %onsite.1, f32[13]{0:T(128)S(1)} %copy-done, f32[1]{0:T(128)S(6)} %copy.7.cut_frac), custom_call_target="tpu_custom_call" | custom-call | tf_op jit(solution)/shard_map/pallas_call | solution.py:579
  91.3 5.5 %shard_map.68 = (f32[512,256]{1,0:T(8,128)}, f32[256,256]{1,0:T(8,128)}, f32[256,256]{1,0:T(8,128)}) custom-call(f32[256,256]{1,0:T(8,128)S(1)} %get-tuple-element.10.gram, f32[512,256]{1,0:T(8,128)S(1)} %get-tuple-element.11.first, f32[256,256]{1,0:T(8,128)S(1)} %get-tuple-element.12.between, f32[256,256]{1,0:T(8,128)S(1)} %get-tuple-element.13.lower_one), custom_call_target="tpu_custom_call" | custom-call | tf_op jit(solution)/shard_map/pallas_call | solution.py:723
Async XLA Ops:
  0.6 0.7 copy-start
